TPU v7x, 32 devices: a whole 2x2x4 slice. The times are simulated.
32 devices in a mesh: dp: 4 (over x, core), fsdp: 8 (over z, y).
Axes of the slice: x: 2, y: 2, z: 4, core: 2. Of those that a mesh axis runs over, the one named last changes fastest.
Arguments:
- latents: float32 [64, 256, 384], P(('dp', 'fsdp')), may hold values from -6 to 6
- condition: float32 [64, 384], P(('dp', 'fsdp')), may hold values from -6 to 6
- cotangent: float32 [64, 256, 384], P(('dp', 'fsdp')), may hold values from -6 to 6
- validity: int32 [64], P(('dp', 'fsdp')), may hold values 0 or 1
- params: float32 [2659584], P(('dp', 'fsdp')), as said below
- moment_one: float32 [2659584], P(('dp', 'fsdp'))
- moment_two: float32 [2659584], P(('dp', 'fsdp')), as said below
Outputs:
- block_out: float32 [64, 256, 384], P(('dp', 'fsdp'))
- latents_grad: float32 [64, 256, 384], P(('dp', 'fsdp'))
- condition_grad: float32 [64, 384], P(('dp', 'fsdp'))
- param_grad: float32 [2659584], P(('dp', 'fsdp'))
- new_params: float32 [2659584], P(('dp', 'fsdp'))
- new_moment_one: float32 [2659584], P(('dp', 'fsdp'))
- new_moment_two: float32 [2659584], P(('dp', 'fsdp'))
Inputs may be any that keep to these rules, and one draw needn't show every extreme that they name: `params`: each segment of the layout has entries of about the scale of an initialized weight. `moment_two`: positive.
All inputs are finite; a program needn't handle non-finite values. No bound on the sum of `validity` on one device may be relied on, other than what follows from the above.
Results may differ from a plain program's by a relative error of at most 0.02.
The roundings to bfloat16 on the way count: a program that leaves them out, or rounds other values in their place, can miss the bound.
Values may be sent and summed in bfloat16 or wider, within the bound.
No kernel may reach another device: no remote copies, remote signals or barrier semaphores. Data moves between devices by JAX's collectives and lax.ppermute only.
A program may use at most 128 MiB of HBM per device.

v0:
```python
import functools
import jax
import jax.numpy as jnp
from jax import lax
from jax.experimental import pallas as pl
from jax.experimental.pallas import tpu as pltpu
from jax.sharding import PartitionSpec as P


D = 384
FF = 1536
HEADS = 6
HEAD_DIM = 64
STEP = 3
LANES = 128

NORM_EPS = 1e-06
LEARN_RATE = 0.01
BETA_ONE = 0.9
BETA_TWO = 0.999
ADAM_EPS = 1e-08
WEIGHT_DECAY = 0.1
MAX_NORM = 1.0
GELU_COEF = 0.7978845608028654
CUBIC_COEF = 0.044715

VMEM_LIMIT = 52 * 1024 * 1024


BF = jnp.bfloat16
F32 = jnp.float32

ADA0 = 0
QKV0 = ADA0 + D * 6 * D // LANES
PROJ0 = QKV0 + D * 3 * D // LANES
FIRST0 = PROJ0 + D * D // LANES
SECOND0 = FIRST0 + D * FF // LANES
BIAS0 = SECOND0 + FF * D // LANES
BIAS_LEN = 6 * D + 3 * D + FF + D
TOTAL = BIAS0 * LANES + BIAS_LEN
B_ADA, B_QUERY, B_VALUE, B_PROJ, B_FIRST, B_SECOND = 0, 6 * D, 7 * D, 8 * D, 9 * D, 9 * D + FF

MATRICES = ((ADA0, D, 6 * D), (QKV0, D, 3 * D), (PROJ0, D, D), (FIRST0, D, FF), (SECOND0, FF, D))


def nn(a, b):
    return lax.dot_general(a, b, (((1,), (0,)), ((), ())), preferred_element_type=F32)


def nt(a, b):
    return lax.dot_general(a, b, (((1,), (1,)), ((), ())), preferred_element_type=F32)


def tn(a, b):
    return lax.dot_general(a, b, (((0,), (0,)), ((), ())), preferred_element_type=F32)


def silu(v):
    return v / (1.0 + jnp.exp(-v))


def mean_last(v):
    return jnp.sum(v, axis=-1, keepdims=True) * (1.0 / v.shape[-1])


def shard_geometry(devices):
    length = TOTAL // devices
    starts = [(length * i) // LANES for i in range(devices)]
    shifts = [(length * i) % LANES for i in range(devices)]
    counts = [-(-(shifts[i] + length) // LANES) for i in range(devices)]
    rows = -(-(max(counts) + 1) // 16) * 16
    return length, starts, shifts, counts, rows


def step_kernel(
    devices, seq, batch, slots_in, slots_out,
    me_ref, valid_ref, lat_hbm, cond_ref, cot_hbm, *rest,
):
    n_in = len(slots_in)
    pieces = rest[:n_in]
    bo_hbm, lg_hbm, cg_ref = rest[n_in : n_in + 3]
    n_out = len(slots_out)
    outs = rest[n_in + 3 : n_in + 3 + n_out]
    (
        stage, flat, w_ada, w_qkv, w_proj, w_first, w_second, bias,
        normed1, inv1, mixed1, qkv, probs, heads_f, heads_h, projected,
        middle, normed2, inv2, mixed2, slope, gelu_h, mlp_out,
        mod, gmod, gcol, gmlp_h, gpre_h, gmix, cond8, gmod_h,
        lat_ref, cot_ref, bo_ref, lg_ref, sem_lat, sem_cot, sem_bo, sem_lg, sems_in, sems_out,
    ) = rest[n_in + 3 + n_out :]
    gmid, gheads, gproj_h, gqkv_h = middle, mlp_out, gmlp_h, gpre_h
    _, starts, shifts, counts, rows = shard_geometry(devices)
    tokens = batch * seq
    scale = HEAD_DIM ** (-0.5)
    me = me_ref[0]
    core_one = me_ref[1] == 1

    def owner(masks):
        return jnp.bitwise_xor(me, jnp.where(core_one, masks[1], masks[0]))

    copy_lat = pltpu.make_async_copy(lat_hbm, lat_ref, sem_lat)
    copy_cot = pltpu.make_async_copy(cot_hbm, cot_ref, sem_cot)
    copy_bo = pltpu.make_async_copy(bo_ref, bo_hbm, sem_bo)
    copy_lg = pltpu.make_async_copy(lg_ref, lg_hbm, sem_lg)
    copy_lat.start()
    copies = []
    for ref, slots in zip(pieces, slots_in):
        for j, masks in enumerate(slots):
            src = ref if len(slots) == 1 else ref.at[j]
            copies.append(
                pltpu.make_async_copy(src, stage.at[owner(masks)], sems_in.at[len(copies)])
            )
            copies[-1].start()
    copy_cot.start()

    chunk = 256

    def norm_one(i, carry):
        rs = pl.ds(pl.multiple_of(i * chunk, chunk), chunk)
        v = lat_ref[rs, :]
        cen = v - mean_last(v)
        inv = lax.rsqrt(mean_last(cen * cen) + NORM_EPS)
        normed1[rs, :] = cen * inv
        inv1[rs, :] = jnp.broadcast_to(inv, (chunk, LANES))
        return carry

    copy_lat.wait()
    lax.fori_loop(0, tokens // chunk, norm_one, 0)

    for c in copies:
        c.wait()
    for i in range(devices):
        g = starts[i]
        n = counts[i]
        block = stage[i].astype(F32)
        if shifts[i] == 0:
            flat[g : g + n, :] = block[:n]
        else:
            flat[g : g + 1, :] = flat[g : g + 1, :] + block[:1]
            flat[g + 1 : g + n, :] = block[1:n]

    for w, (base, height, width) in zip((w_ada, w_qkv, w_proj, w_first, w_second), MATRICES):
        tiles = width // LANES
        for c in range(tiles):
            w[:, c * LANES : (c + 1) * LANES] = flat[pl.ds(base + c, height, stride=tiles), :].astype(BF)
    for r in range(BIAS_LEN // LANES):
        bias[:, r * LANES : (r + 1) * LANES] = flat[BIAS0 + r : BIAS0 + r + 1, :]

    cond8[...] = jnp.zeros_like(cond8)
    cond8[0:batch, :] = silu(cond_ref[...])
    ch = cond8[...].astype(BF)
    mod[...] = nn(ch, w_ada[...]) + bias[:, B_ADA : B_ADA + 6 * D]

    def part(ref, b, k):
        return ref[pl.ds(b, 1), k * D : (k + 1) * D]

    def mix_one(i, carry):
        b = i // (seq // chunk)
        rs = pl.ds(pl.multiple_of(i * chunk, chunk), chunk)
        mixed1[rs, :] = (normed1[rs, :] * (1.0 + part(mod, b, 1)) + part(mod, b, 0)).astype(BF)
        return carry

    lax.fori_loop(0, tokens // chunk, mix_one, 0)

    for j in range(3):
        cols = slice(j * D, (j + 1) * D)
        acc = nn(mixed1[...], w_qkv[:, cols])
        if j == 0:
            acc = acc + bias[:, B_QUERY : B_QUERY + D]
        if j == 2:
            acc = acc + bias[:, B_VALUE : B_VALUE + D]
        qkv[:, cols] = acc.astype(BF)

    lane = lax.broadcasted_iota(jnp.int32, (1, LANES), 1)
    low = lane < HEAD_DIM
    zero_bf = jnp.zeros((), BF)

    def keep(v, half):
        return jnp.where(low if half == 0 else jnp.logical_not(low), v, zero_bf)

    pairs = HEADS // 2

    def attn(b, carry):
        rs = pl.ds(pl.multiple_of(b * seq, seq), seq)
        for h in range(pairs):
            q = qkv[rs, h * LANES : (h + 1) * LANES]
            k = qkv[rs, D + h * LANES : D + (h + 1) * LANES]
            v = qkv[rs, 2 * D + h * LANES : 2 * D + (h + 1) * LANES]
            res = []
            for half in range(2):
                s = nt(keep(q, half), k) * scale
                e = jnp.exp(s - jnp.max(s, axis=-1, keepdims=True))
                p = e * (1.0 / jnp.sum(e, axis=-1, keepdims=True))
                probs[b * HEADS + 2 * h + half] = p
                res.append(nn(p.astype(BF), v))
            o = jnp.where(low, res[0], res[1])
            heads_f[rs, h * LANES : (h + 1) * LANES] = o
            heads_h[rs, h * LANES : (h + 1) * LANES] = o.astype(BF)
        return carry

    lax.fori_loop(0, batch, attn, 0)

    projected[...] = nn(heads_h[...], w_proj[...]) + bias[:, B_PROJ : B_PROJ + D]

    def mid(i, carry):
        b = i // (seq // chunk)
        rs = pl.ds(pl.multiple_of(i * chunk, chunk), chunk)
        m = lat_ref[rs, :] + part(mod, b, 2) * projected[rs, :]
        middle[rs, :] = m
        cen = m - mean_last(m)
        inv = lax.rsqrt(mean_last(cen * cen) + NORM_EPS)
        n2 = cen * inv
        normed2[rs, :] = n2
        inv2[rs, :] = jnp.broadcast_to(inv, (chunk, LANES))
        mixed2[rs, :] = (n2 * (1.0 + part(mod, b, 4)) + part(mod, b, 3)).astype(BF)
        return carry

    lax.fori_loop(0, tokens // chunk, mid, 0)

    fchunk = 256
    for j in range(FF // fchunk):
        cols = slice(j * fchunk, (j + 1) * fchunk)
        u = nn(mixed2[...], w_first[:, cols]) + bias[:, B_FIRST + j * fchunk : B_FIRST + (j + 1) * fchunk]
        uu = u * u
        t = jnp.tanh(GELU_COEF * (u + CUBIC_COEF * uu * u))
        half_u = 0.5 * u
        gelu_h[:, cols] = (half_u * (1.0 + t)).astype(BF)
        slope[:, cols] = 0.5 * (1.0 + t) + half_u * (1.0 - t * t) * GELU_COEF * (
            1.0 + 3.0 * CUBIC_COEF * uu
        )
    mlp_out[...] = nn(gelu_h[...], w_second[...]) + bias[:, B_SECOND : B_SECOND + D]

    gcol[...] = jnp.zeros_like(gcol)
    gmod[...] = jnp.zeros_like(gmod)

    def add_col(ref, b, k, v):
        ref[pl.ds(b, 1), k * D : (k + 1) * D] += jnp.sum(v, axis=0, keepdims=True)

    def out_step(i, carry):
        b = i // (seq // chunk)
        rs = pl.ds(pl.multiple_of(i * chunk, chunk), chunk)
        mo = mlp_out[rs, :]
        gate = part(mod, b, 5)
        bo_ref[rs, :] = middle[rs, :] + gate * mo
        up = cot_ref[rs, :] * valid_ref[b].astype(F32)
        add_col(gmod, b, 5, up * mo)
        gm = up * gate
        gcol[:, B_SECOND : B_SECOND + D] += jnp.sum(gm, axis=0, keepdims=True)
        gmlp_h[rs, :] = gm.astype(BF)
        return carry

    copy_cot.wait()
    lax.fori_loop(0, tokens // chunk, out_step, 0)
    copy_bo.start()

    def put(base, tiles, height, row0, c0, value):
        for c in range(value.shape[1] // LANES):
            flat[pl.ds(base + row0 * tiles + c0 + c, height, stride=tiles), :] = value[
                :, c * LANES : (c + 1) * LANES
            ]

    for j in range(FF // D):
        rr = slice(j * D, (j + 1) * D)
        put(SECOND0, D // LANES, D, j * D, 0, tn(gelu_h[:, rr], gmlp_h[...]))
    for j in range(FF // fchunk):
        cols = slice(j * fchunk, (j + 1) * fchunk)
        gp = nt(gmlp_h[...], w_second[cols, :]) * slope[:, cols]
        gcol[:, B_FIRST + j * fchunk : B_FIRST + (j + 1) * fchunk] = jnp.sum(gp, axis=0, keepdims=True)
        gpre_h[:, cols] = gp.astype(BF)
    for j in range(FF // D):
        cols = slice(j * D, (j + 1) * D)
        put(FIRST0, FF // LANES, D, 0, j * (D // LANES), tn(mixed2[...], gpre_h[:, cols]))
    gmix[...] = nt(gpre_h[...], w_first[...])

    def back_two(i, carry):
        b = i // (seq // chunk)
        rs = pl.ds(pl.multiple_of(i * chunk, chunk), chunk)
        g = gmix[rs, :]
        n2 = normed2[rs, :]
        add_col(gmod, b, 3, g)
        add_col(gmod, b, 4, g * n2)
        e = g * (1.0 + part(mod, b, 4))
        up = cot_ref[rs, :] * valid_ref[b].astype(F32)
        inv = inv2[rs, 0:1]
        gm = up + inv * (e - mean_last(e) - n2 * mean_last(e * n2))
        gmid[rs, :] = gm
        add_col(gmod, b, 2, gm * projected[rs, :])
        gp = gm * part(mod, b, 2)
        gcol[:, B_PROJ : B_PROJ + D] += jnp.sum(gp, axis=0, keepdims=True)
        gproj_h[rs, :] = gp.astype(BF)
        return carry

    lax.fori_loop(0, tokens // chunk, back_two, 0)

    put(PROJ0, D // LANES, D, 0, 0, tn(heads_h[...], gproj_h[...]))
    gheads[...] = nt(gproj_h[...], w_proj[...])

    def attn_back(b, carry):
        rs = pl.ds(pl.multiple_of(b * seq, seq), seq)
        for h in range(pairs):
            ls = slice(h * LANES, (h + 1) * LANES)
            q = qkv[rs, h * LANES : (h + 1) * LANES]
            k = qkv[rs, D + h * LANES : D + (h + 1) * LANES]
            v = qkv[rs, 2 * D + h * LANES : 2 * D + (h + 1) * LANES]
            gh = gheads[rs, ls]
            prod = gh * heads_f[rs, ls]
            ghh = gh.astype(BF)
            dq, dk, dv = [], [], []
            for half in range(2):
                delta = jnp.sum(
                    jnp.where(low if half == 0 else jnp.logical_not(low), prod, 0.0),
                    axis=-1, keepdims=True,
                )
                p = probs[b * HEADS + 2 * h + half]
                gp = nt(keep(ghh, half), v)
                gs = (p * (gp - delta)).astype(BF)
                dq.append(nn(gs, k))
                dk.append(tn(gs, q))
                dv.append(tn(p.astype(BF), ghh))
            gq = jnp.where(low, dq[0], dq[1]) * scale
            gk = jnp.where(low, dk[0], dk[1]) * scale
            gv = jnp.where(low, dv[0], dv[1])
            gcol[:, B_QUERY + h * LANES : B_QUERY + (h + 1) * LANES] += jnp.sum(gq, axis=0, keepdims=True)
            gcol[:, B_VALUE + h * LANES : B_VALUE + (h + 1) * LANES] += jnp.sum(gv, axis=0, keepdims=True)
            gqkv_h[rs, h * LANES : (h + 1) * LANES] = gq.astype(BF)
            gqkv_h[rs, D + h * LANES : D + (h + 1) * LANES] = gk.astype(BF)
            gqkv_h[rs, 2 * D + h * LANES : 2 * D + (h + 1) * LANES] = gv.astype(BF)
        return carry

    lax.fori_loop(0, batch, attn_back, 0)

    for j in range(3):
        cols = slice(j * D, (j + 1) * D)
        put(QKV0, 3 * D // LANES, D, 0, j * (D // LANES), tn(mixed1[...], gqkv_h[:, cols]))
    gmix[...] = nt(gqkv_h[:, : 3 * D], w_qkv[...])

    def back_one(i, carry):
        b = i // (seq // chunk)
        rs = pl.ds(pl.multiple_of(i * chunk, chunk), chunk)
        g = gmix[rs, :]
        n1 = normed1[rs, :]
        add_col(gmod, b, 0, g)
        add_col(gmod, b, 1, g * n1)
        e = g * (1.0 + part(mod, b, 1))
        inv = inv1[rs, 0:1]
        lg_ref[rs, :] = gmid[rs, :] + inv * (e - mean_last(e) - n1 * mean_last(e * n1))
        return carry

    lax.fori_loop(0, tokens // chunk, back_one, 0)
    copy_lg.start()

    gmod_h[...] = gmod[...].astype(BF)
    for j in range(6):
        cols = slice(j * D, (j + 1) * D)
        put(ADA0, 6 * D // LANES, D, 0, j * (D // LANES), tn(ch, gmod_h[:, cols]))
    gcol[:, B_ADA : B_ADA + 6 * D] = jnp.sum(gmod[...], axis=0, keepdims=True)
    cg = nt(gmod_h[...], w_ada[...])[0:batch]
    cv = cond_ref[...]
    sig = 1.0 / (1.0 + jnp.exp(-cv))
    cg_ref[...] = cg * (sig * (1.0 + cv * (1.0 - sig)))

    for r in range(BIAS_LEN // LANES):
        flat[BIAS0 + r : BIAS0 + r + 1, :] = gcol[:, r * LANES : (r + 1) * LANES]

    for i in range(devices):
        g = starts[i]
        stage[i] = flat[g : g + rows, :].astype(BF)
    copies = [copy_bo, copy_lg]
    for ref, slots in zip(outs, slots_out):
        for j, masks in enumerate(slots):
            copies.append(
                pltpu.make_async_copy(stage.at[owner(masks)], ref.at[j], sems_out.at[len(copies) - 2])
            )
            copies[-1].start()
    for c in copies:
        c.wait()


def run_step(
    devices, place, validity, latents, condition, cotangent, pieces, slots_in, slots_out
):
    batch, seq, _ = latents.shape
    tokens = batch * seq
    _, starts, _, _, rows = shard_geometry(devices)
    flat_rows = -(-(starts[-1] + rows) // 16) * 16
    vm = pl.BlockSpec(memory_space=pltpu.VMEM)
    hb = pl.BlockSpec(memory_space=pl.ANY)
    sm = pl.BlockSpec(memory_space=pltpu.SMEM)
    out_shape = [
        jax.ShapeDtypeStruct((tokens, D), F32),
        jax.ShapeDtypeStruct((tokens, D), F32),
        jax.ShapeDtypeStruct((batch, D), F32),
    ] + [
        jax.ShapeDtypeStruct((len(slots), rows, LANES), BF) for slots in slots_out
    ]
    V = pltpu.VMEM
    scratch = [
        V((devices, rows, LANES), BF),
        V((flat_rows, LANES), F32),
        V((D, 6 * D), BF), V((D, 3 * D), BF), V((D, D), BF), V((D, FF), BF), V((FF, D), BF),
        V((1, BIAS_LEN), F32),
        V((tokens, D), F32), V((tokens, LANES), F32), V((tokens, D), BF), V((tokens, 3 * D), BF),
        V((batch * HEADS, seq, seq), F32), V((tokens, D), F32), V((tokens, D), BF), V((tokens, D), F32),
        V((tokens, D), F32), V((tokens, D), F32), V((tokens, LANES), F32), V((tokens, D), BF),
        V((tokens, FF), F32), V((tokens, FF), BF), V((tokens, D), F32),
        V((8, 6 * D), F32), V((8, 6 * D), F32), V((1, BIAS_LEN), F32),
        V((tokens, D), BF), V((tokens, FF), BF), V((tokens, D), F32), V((8, D), F32), V((8, 6 * D), BF),
        V((tokens, D), F32), V((tokens, D), F32), V((tokens, D), F32), V((tokens, D), F32),
        pltpu.SemaphoreType.DMA, pltpu.SemaphoreType.DMA, pltpu.SemaphoreType.DMA, pltpu.SemaphoreType.DMA,
        pltpu.SemaphoreType.DMA((devices,)), pltpu.SemaphoreType.DMA((devices,)),
    ]
    body = functools.partial(step_kernel, devices, seq, batch, slots_in, slots_out)
    res = pl.pallas_call(
        body,
        out_shape=out_shape,
        in_specs=[sm, sm, hb, vm, hb] + [hb] * len(pieces),
        out_specs=[hb, hb, vm] + [hb] * len(slots_out),
        scratch_shapes=scratch,
        compiler_params=pltpu.CompilerParams(vmem_limit_bytes=VMEM_LIMIT),
        name="step",
    )(
        place, validity, latents.reshape(tokens, D), condition, cotangent.reshape(tokens, D), *pieces
    )
    return res[0], res[1], res[2], res[3:]


def shift_kernel(s_ref, x_ref, o_ref):
    s = s_ref[0]
    rolled = pltpu.roll(x_ref[...], s, 1)
    above = pltpu.roll(rolled, 1, 0)
    lane = lax.broadcasted_iota(jnp.int32, rolled.shape, 1)
    o_ref[...] = jnp.where(lane < s, above, rolled).astype(BF)


def shift_shard(shift, params, rows):
    padded = jnp.pad(params, (0, rows * LANES - params.shape[0])).reshape(rows, LANES)
    return pl.pallas_call(
        shift_kernel,
        out_shape=jax.ShapeDtypeStruct((rows, LANES), BF),
        in_specs=[pl.BlockSpec(memory_space=pltpu.SMEM), pl.BlockSpec(memory_space=pltpu.VMEM)],
        out_specs=pl.BlockSpec(memory_space=pltpu.VMEM),
        name="shift",
    )(shift, padded)


def unshift_kernel(length, n, s_ref, *refs):
    s = s_ref[0]
    total = refs[0][...].astype(F32)
    for r in refs[1:n]:
        total = total + r[...].astype(F32)
    g_ref, sq_ref = refs[n:]
    rows = total.shape[0]
    back = jnp.where(s == 0, 0, LANES - s)
    rolled = pltpu.roll(total, back, 1)
    below = pltpu.roll(rolled, rows - 1, 0)
    lane = lax.broadcasted_iota(jnp.int32, rolled.shape, 1)
    row = lax.broadcasted_iota(jnp.int32, rolled.shape, 0)
    out = jnp.where(lane < LANES - s, rolled, below)
    out = jnp.where(row * LANES + lane < length, out, 0.0)
    g_ref[...] = out
    sq_ref[...] = jnp.full(sq_ref.shape, jnp.sum(out * out), F32)


def unshift(shift, parts, length):
    rows = parts[0].shape[0]
    return pl.pallas_call(
        functools.partial(unshift_kernel, length, len(parts)),
        out_shape=[jax.ShapeDtypeStruct((rows, LANES), F32), jax.ShapeDtypeStruct((8, LANES), F32)],
        in_specs=[pl.BlockSpec(memory_space=pltpu.SMEM)]
        + [pl.BlockSpec(memory_space=pltpu.VMEM)] * len(parts),
        out_specs=[pl.BlockSpec(memory_space=pltpu.VMEM)] * 2,
        name="unshift",
    )(shift, *parts)


HOPS = {"a": 16, "b": 1, "z1": 2, "z2": 4, "z3": 6}
GATHER = (
    (16, "a"), (4, "z2"), (1, "b"), (2, "z1"), (18, "z1"), (22, "z3"), (17, "a"), (7, "z3"),
    (5, "b"), (20, "a"), (19, "z1"), (3, "b"), (21, "a"), (6, "z1"), (23, "b"),
)
SCATTER = (
    (23, "z3"), (20, "a"), (7, "z1"), (21, "a"), (3, "b"), (19, "z1"), (6, "z1"), (22, "z3"),
    (5, "b"), (18, "a"), (17, "b"), (4, "z2"), (2, "z1"), (1, "b"), (16, "a"),
)
GATHER_NODES = (0,) + tuple(n for n, _ in GATHER)
SCATTER_NODES = tuple(n for n, _ in SCATTER) + (0,)
GROUP = 4


def swap(node):
    return (node & 6) | (16 if node & 1 else 0) | (1 if node & 16 else 0)


def hop(v, kind):
    pairs = []
    for i in range(32):
        m = 8 if kind == "core" else HOPS[kind]
        pairs.append((i, i ^ (swap(m) if i & 8 and kind != "core" else m)))
    return lax.ppermute(v, ("dp", "fsdp"), pairs)


def near(nodes):
    return [(n, swap(n)) for n in nodes]


def far(nodes):
    return [(8 ^ swap(n), 8 ^ n) for n in nodes]


def local(latents, condition, cotangent, validity, params, moment_one, moment_two):
    outer = lax.axis_size("dp")
    inner = lax.axis_size("fsdp")
    devices = outer * inner
    both = ("dp", "fsdp")
    me = (lax.axis_index("dp") * inner + lax.axis_index("fsdp")).astype(jnp.int32)
    length, _, _, _, rows = shard_geometry(devices)
    shift = ((me * (length % LANES)) % LANES).astype(jnp.int32).reshape(1)
    own = shift_shard(shift, params, rows)
    if (outer, inner) == (4, 8):
        core = jnp.bitwise_and(jnp.right_shift(me, 3), 1)
        place = jnp.stack([me, core])
        got = {0: own}
        for node, kind in GATHER:
            got[node] = hop(got[node ^ HOPS[kind]], kind)
        pieces = [got[n] for n in GATHER_NODES]
        crossed = []
        for v in pieces:
            crossed.append(hop(v, "core"))
        cuts = [SCATTER_NODES[k : k + GROUP] for k in range(0, len(SCATTER_NODES), GROUP)]
        bo, lg, cg, blocks = run_step(
            devices, place, validity, latents, condition, cotangent, pieces + crossed,
            [[m] for m in near(GATHER_NODES) + far(GATHER_NODES)],
            [near(c) for c in cuts] + [far(c) for c in cuts],
        )
        sums = {}
        for j, cut in enumerate(cuts):
            theirs = hop(blocks[len(cuts) + j], "core")
            for k, node in enumerate(cut):
                sums[node] = (blocks[j][k].astype(F32) + theirs[k].astype(F32)).astype(BF)
        waiting = {n: [] for n in SCATTER_NODES}
        for node, kind in SCATTER:
            half = sums[node]
            if waiting[node]:
                half = half.astype(F32)
                for extra in waiting[node]:
                    half = half + extra.astype(F32)
                half = half.astype(BF)
            waiting[node ^ HOPS[kind]].append(hop(half, kind))
        parts = [sums[0]] + waiting[0]
    else:
        gathered = lax.all_gather(own, both, axis=0, tiled=False)
        every = [[(i, i) for i in range(devices)]]
        bo, lg, cg, (chunks,) = run_step(
            devices, jnp.zeros((2,), jnp.int32), validity, latents, condition, cotangent,
            [gathered], every, every,
        )
        parts = [lax.psum_scatter(chunks, both, scatter_dimension=0, tiled=False)]
    grad, squares = unshift(shift, parts, length)
    for axis, size in (("dp", outer), ("fsdp", inner)):
        d = 1
        while d < size:
            squares = squares + lax.ppermute(squares, axis, [(i, i ^ d) for i in range(size)])
            d *= 2
    clip_factor = jnp.minimum(1.0, MAX_NORM / (jnp.sqrt(squares[0, 0]) + NORM_EPS))
    grad_shard = grad.reshape(-1)[:length]
    clipped = grad_shard * clip_factor
    new_one = BETA_ONE * moment_one + (1.0 - BETA_ONE) * clipped
    new_two = BETA_TWO * moment_two + (1.0 - BETA_TWO) * clipped * clipped
    corrected_one = new_one / (1.0 - BETA_ONE**STEP)
    corrected_two = new_two / (1.0 - BETA_TWO**STEP)
    new_params = params - LEARN_RATE * (
        corrected_one / (jnp.sqrt(corrected_two) + ADAM_EPS) + WEIGHT_DECAY * params
    )
    return (
        bo.reshape(latents.shape), lg.reshape(latents.shape), cg,
        grad_shard, new_params, new_one, new_two,
    )


def solution(mesh):
    both = ("dp", "fsdp")
    in_specs = (
        P(both, None, None), P(both, None), P(both, None, None),
        P(both), P(both), P(both), P(both),
    )
    out_specs = (
        P(both, None, None), P(both, None, None), P(both, None),
        P(both), P(both), P(both), P(both),
    )
    return jax.shard_map(local, mesh=mesh, in_specs=in_specs, out_specs=out_specs, check_vma=False)
```

profile of v0, /device:TPU:0, one launch (start us, length us, event | category | flops | bytes accessed | tf_op | source)
XLA Modules:
  0.0 150.7 jit_solution(8269677182796795336)
XLA Ops:
  4.1 3.1 %collective-permute-start.3 = (bf16[656,128]{1,0:T(8,128)(2,1)}, bf16[656,128]{1,0:T(8,128)(2,1)S(1)}, u32[]{:S(2)}, u32[]{:S(2)}) collective-permute-start(bf16[656,128]{1,0:T(8,128)(2,1)} %shift.1.rest_0_), channel_id=1, source_target_pairs={{0,2},{1,3},{2,0},{3,1},{4,6},{5,7},{6,4},{7,5},{8,10},{9,11},{10,... | collective-permute-start | bytes 503816 | tf_op jit(solution)/shard_map/ppermute | solution.py:499
  8.7 2.6 %collective-permute-start.1 = (bf16[656,128]{1,0:T(8,128)(2,1)}, bf16[656,128]{1,0:T(8,128)(2,1)S(1)}, u32[]{:S(2)}, u32[]{:S(2)}) collective-permute-start(bf16[656,128]{1,0:T(8,128)(2,1)} %shift.1.rest_0_), channel_id=1, source_target_pairs={{0,4},{1,5},{2,6},{3,7},{4,0},{5,1},{6,2},{7,3},{8,12},{9,13},{10,... | collective-permute-start | bytes 503816 | tf_op jit(solution)/shard_map/ppermute | solution.py:499
  14.7 5.1 %collective-permute-done.1.rest_2_ = bf16[656,128]{1,0:T(8,128)(2,1)S(1)} collective-permute-done((bf16[656,128]{1,0:T(8,128)(2,1)}, bf16[656,128]{1,0:T(8,128)(2,1)S(1)}, u32[]{:S(2)}, u32[]{:S(2)}) %collective-permute-start.1) | collective-permute-done | bytes 167968 | tf_op jit(solution)/shard_map/ppermute | solution.py:499
  19.8 2.5 %collective-permute-start.7 = (bf16[656,128]{1,0:T(8,128)(2,1)S(1)}, bf16[656,128]{1,0:T(8,128)(2,1)S(1)}, u32[]{:S(2)}, u32[]{:S(2)}) collective-permute-start(bf16[656,128]{1,0:T(8,128)(2,1)S(1)} %collective-permute-done.2.rest_3_), channel_id=1, source_target_pairs={{0,6},{1,7},{2,4},{3,5},{4,2},{5,3},{6,0},{7,1},{8,14},{9,15},{10,... | collective-permute-start | bytes 503816 | tf_op jit(solution)/shard_map/ppermute | solution.py:499
  24.6 4.2 %collective-permute-done.7.rest_8_ = bf16[656,128]{1,0:T(8,128)(2,1)S(1)} collective-permute-done((bf16[656,128]{1,0:T(8,128)(2,1)S(1)}, bf16[656,128]{1,0:T(8,128)(2,1)S(1)}, u32[]{:S(2)}, u32[]{:S(2)}) %collective-permute-start.7) | collective-permute-done | bytes 167968 | tf_op jit(solution)/shard_map/ppermute | solution.py:499
  29.9 2.6 %collective-permute-start.5 = (bf16[656,128]{1,0:T(8,128)(2,1)S(1)}, bf16[656,128]{1,0:T(8,128)(2,1)S(1)}, u32[]{:S(2)}, u32[]{:S(2)}) collective-permute-start(bf16[656,128]{1,0:T(8,128)(2,1)S(1)} %collective-permute-done.rest_1_), channel_id=1, source_target_pairs={{0,6},{1,7},{2,4},{3,5},{4,2},{5,3},{6,0},{7,1},{8,14},{9,15},{10,... | collective-permute-start | bytes 503816 | tf_op jit(solution)/shard_map/ppermute | solution.py:499
  34.7 4.3 %collective-permute-done.5.rest_6_ = bf16[656,128]{1,0:T(8,128)(2,1)S(1)} collective-permute-done((bf16[656,128]{1,0:T(8,128)(2,1)S(1)}, bf16[656,128]{1,0:T(8,128)(2,1)S(1)}, u32[]{:S(2)}, u32[]{:S(2)}) %collective-permute-start.5) | collective-permute-done | bytes 167968 | tf_op jit(solution)/shard_map/ppermute | solution.py:499
  39.0 2.2 %collective-permute-start.10 = (bf16[656,128]{1,0:T(8,128)(2,1)S(1)}, bf16[656,128]{1,0:T(8,128)(2,1)S(1)}, u32[]{:S(2)}, u32[]{:S(2)}) collective-permute-start(bf16[656,128]{1,0:T(8,128)(2,1)S(1)} %collective-permute-done.6.rest_7_), channel_id=1, source_target_pairs={{0,2},{1,3},{2,0},{3,1},{4,6},{5,7},{6,4},{7,5},{8,10},{9,11},{10,... | collective-permute-start | bytes 503816 | tf_op jit(solution)/shard_map/ppermute | solution.py:499
  43.6 2.0 %collective-permute-done.10.rest_11_ = bf16[656,128]{1,0:T(8,128)(2,1)S(1)} collective-permute-done((bf16[656,128]{1,0:T(8,128)(2,1)S(1)}, bf16[656,128]{1,0:T(8,128)(2,1)S(1)}, u32[]{:S(2)}, u32[]{:S(2)}) %collective-permute-start.10) | collective-permute-done | bytes 167968 | tf_op jit(solution)/shard_map/ppermute | solution.py:499
  48.6 2.6 %collective-permute-done.14.rest_15_ = bf16[656,128]{1,0:T(8,128)(2,1)} collective-permute-done((bf16[656,128]{1,0:T(8,128)(2,1)S(1)}, bf16[656,128]{1,0:T(8,128)(2,1)}, u32[]{:S(2)}, u32[]{:S(2)}) %collective-permute-start.14) | collective-permute-done | bytes 167968 | tf_op jit(solution)/shard_map/ppermute | solution.py:499
  54.5 31.5 %step.1 = (f32[512,384]{1,0:T(8,128)}, f32[512,384]{1,0:T(8,128)}, f32[2,384]{1,0:T(2,128)}, bf16[4,656,128]{2,1,0:T(8,128)(2,1)}, bf16[4,656,128]{2,1,0:T(8,128...) custom-call(s32[2]{0:T(128)S(1)} %pad_add_fusion.me_ref, ...), custom_call_target="tpu_custom_call" | custom-call | tf_op jit(solution)/shard_map/step/pallas_call | solution.py:413
  92.6 2.1 %collective-permute-start.47 = (bf16[656,128]{1,0:T(8,128)(2,1)S(1)}, bf16[656,128]{1,0:T(8,128)(2,1)S(1)}, u32[]{:S(2)}, u32[]{:S(2)}) collective-permute-start(bf16[656,128]{1,0:T(8,128)(2,1)S(1)} %get-tuple-element.40), channel_id=1, source_target_pairs={{0,2},{1,3},{2,0},{3,1},{4,6},{5,7},{6,4},{7,5},{8,10},{9,11},{10,... | collective-permute-start | bytes 503816 | tf_op jit(solution)/shard_map/ppermute | solution.py:499
  94.8 4.1 %collective-permute-done.46 = bf16[656,128]{1,0:T(8,128)(2,1)S(1)} collective-permute-done((bf16[656,128]{1,0:T(8,128)(2,1)S(1)}, bf16[656,128]{1,0:T(8,128)(2,1)S(1)}, u32[]{:S(2)}, u32[]{:S(2)}) %collective-permute-start.46) | collective-permute-done | bytes 167968 | tf_op jit(solution)/shard_map/ppermute | solution.py:499
  102.8 3.4 %collective-permute-done.47 = bf16[656,128]{1,0:T(8,128)(2,1)S(1)} collective-permute-done((bf16[656,128]{1,0:T(8,128)(2,1)S(1)}, bf16[656,128]{1,0:T(8,128)(2,1)S(1)}, u32[]{:S(2)}, u32[]{:S(2)}) %collective-permute-start.47) | collective-permute-done | bytes 167968 | tf_op jit(solution)/shard_map/ppermute | solution.py:499
  113.3 2.9 %collective-permute-done.34 = bf16[656,128]{1,0:T(8,128)(2,1)S(1)} collective-permute-done((bf16[656,128]{1,0:T(8,128)(2,1)S(1)}, bf16[656,128]{1,0:T(8,128)(2,1)S(1)}, u32[]{:S(2)}, u32[]{:S(2)}) %collective-permute-start.34) | collective-permute-done | bytes 167968 | tf_op jit(solution)/shard_map/ppermute | solution.py:499
  116.1 2.8 %collective-permute-done.39 = bf16[656,128]{1,0:T(8,128)(2,1)S(1)} collective-permute-done((bf16[656,128]{1,0:T(8,128)(2,1)S(1)}, bf16[656,128]{1,0:T(8,128)(2,1)S(1)}, u32[]{:S(2)}, u32[]{:S(2)}) %collective-permute-start.39) | collective-permute-done | bytes 167968 | tf_op jit(solution)/shard_map/ppermute | solution.py:499
  119.6 3.4 %collective-permute-done.43.refs_2_ = bf16[656,128]{1,0:T(8,128)(2,1)S(1)} collective-permute-done((bf16[656,128]{1,0:T(8,128)(2,1)S(1)}, bf16[656,128]{1,0:T(8,128)(2,1)S(1)}, u32[]{:S(2)}, u32[]{:S(2)}) %collective-permute-start.43) | collective-permute-done | bytes 167968 | tf_op jit(solution)/shard_map/ppermute | solution.py:499
  123.0 3.9 %collective-permute-done.40.refs_1_ = bf16[656,128]{1,0:T(8,128)(2,1)S(1)} collective-permute-done((bf16[656,128]{1,0:T(8,128)(2,1)S(1)}, bf16[656,128]{1,0:T(8,128)(2,1)S(1)}, u32[]{:S(2)}, u32[]{:S(2)}) %collective-permute-start.40) | collective-permute-done | bytes 167968 | tf_op jit(solution)/shard_map/ppermute | solution.py:499
  127.6 2.2 %unshift.1 = (f32[656,128]{1,0:T(8,128)}, f32[8,128]{1,0:T(8,128)}) custom-call(s32[1]{0:T(128)} %bitcast.4.s_ref, bf16[656,128]{1,0:T(8,128)(2,1)} %get-tuple-element.50.refs_0_, bf16[656,128]{1,0:T(8,128)(2,1)} %copy-done.12, bf16[656,128]{1,0:T(8,128)(2,1)} %copy-done.11, bf16[656,128]{1,0:T(8,128)(2,1)} %copy-done.9, bf16[656,128]{1,0:T(8,128)(2,1)} %copy-done.10), custom_call_target="tpu_custom_call" | custom-call | tf_op jit(solution)/shard_map/unshift/pallas_call | solution.py:466
  132.6 2.9 %collective-permute-done.51 = f32[8,128]{1,0:T(8,128)S(1)} collective-permute-done((f32[8,128]{1,0:T(8,128)S(1)}, f32[8,128]{1,0:T(8,128)S(1)}, u32[]{:S(2)}, u32[]{:S(2)}) %collective-permute-start.51) | collective-permute-done | bytes 4128 | tf_op jit(solution)/shard_map/ppermute | solution.py:562
  136.8 2.3 %collective-permute-done.52 = f32[8,128]{1,0:T(8,128)S(1)} collective-permute-done((f32[8,128]{1,0:T(8,128)S(1)}, f32[8,128]{1,0:T(8,128)S(1)}, u32[]{:S(2)}, u32[]{:S(2)}) %collective-permute-start.52) | collective-permute-done | bytes 4128 | tf_op jit(solution)/shard_map/ppermute | solution.py:562
  139.1 3.6 %collective-permute-done.53 = f32[8,128]{1,0:T(8,128)S(1)} collective-permute-done((f32[8,128]{1,0:T(8,128)S(1)}, f32[8,128]{1,0:T(8,128)S(1)}, u32[]{:S(2)}, u32[]{:S(2)}) %collective-permute-start.53) | collective-permute-done | bytes 4128 | tf_op jit(solution)/shard_map/ppermute | solution.py:562
  143.1 4.2 %collective-permute-done.54 = f32[8,128]{1,0:T(8,128)S(1)} collective-permute-done((f32[8,128]{1,0:T(8,128)S(1)}, f32[8,128]{1,0:T(8,128)S(1)}, u32[]{:S(2)}, u32[]{:S(2)}) %collective-permute-start.54) | collective-permute-done | bytes 4128 | tf_op jit(solution)/shard_map/ppermute | solution.py:562
  148.5 2.1 %multiply_subtract_fusion = (f32[83112]{0:T(1024)}, f32[83112]{0:T(1024)}, f32[83112]{0:T(1024)}, f32[83112]{0:T(1024)}) fusion(f32[83112]{0:T(1024)S(1)} %copy-done.3, f32[]{:T(128)} %bitcast.25, f32[83112]{0:T(1024)S(1)} %copy-done.7, f32[83112]{0:T(1024)S(1)} %copy-done.8, f32[83968]{0:T(1024)} %bitcast.60), kind=kLoop, calls=%fused_computation.18 | loop fusion | flops 1329792 | bytes 2659588 | tf_op jit(solution)/shard_map/sub | solution.py:571
  (157 shorter events, 46.5 us)
Async XLA Ops:
  4.1 8.7 %collective-permute-start.3 = (bf16[656,128]{1,0:T(8,128)(2,1)}, bf16[656,128]{1,0:T(8,128)(2,1)S(1)}, u32[]{:S(2)}, u32[]{:S(2)}) collective-permute-start(bf16[656,128]{1,0:T(8,128)(2,1)} %shift.1.rest_0_), channel_id=1, source_target_pairs={{0,2},{1,3},{2,0},{3,1},{4,6},{5,7},{6,4},{7,5},{8,10},{9,11},{10,... | collective-permute-start | bytes 503816 | tf_op jit(solution)/shard_map/ppermute | solution.py:499
  8.7 11.1 %collective-permute-start.1 = (bf16[656,128]{1,0:T(8,128)(2,1)}, bf16[656,128]{1,0:T(8,128)(2,1)S(1)}, u32[]{:S(2)}, u32[]{:S(2)}) collective-permute-start(bf16[656,128]{1,0:T(8,128)(2,1)} %shift.1.rest_0_), channel_id=1, source_target_pairs={{0,4},{1,5},{2,6},{3,7},{4,0},{5,1},{6,2},{7,3},{8,12},{9,13},{10,... | collective-permute-start | bytes 503816 | tf_op jit(solution)/shard_map/ppermute | solution.py:499
  11.3 11.0 %collective-permute-start = (bf16[656,128]{1,0:T(8,128)(2,1)}, bf16[656,128]{1,0:T(8,128)(2,1)S(1)}, u32[]{:S(2)}, u32[]{:S(2)}) collective-permute-start(bf16[656,128]{1,0:T(8,128)(2,1)} %shift.1.rest_0_), channel_id=1, source_target_pairs={{0,16},{1,17},{2,18},{3,19},{4,20},{5,21},{6,22},{7,23},{8,9},{9,8... | collective-permute-start | bytes 503816 | tf_op jit(solution)/shard_map/ppermute | solution.py:499
  12.8 10.3 %collective-permute-start.19 = (bf16[656,128]{1,0:T(8,128)(2,1)S(1)}, bf16[656,128]{1,0:T(8,128)(2,1)S(1)}, u32[]{:S(2)}, u32[]{:S(2)}) collective-permute-start(bf16[656,128]{1,0:T(8,128)(2,1)S(1)} %collective-permute-done.3.rest_4_), channel_id=1, source_target_pairs={{0,8},{1,9},{2,10},{3,11},{4,12},{5,13},{6,14},{7,15},{8,0},{9,1},... | collective-permute-start | bytes 503816 | tf_op jit(solution)/shard_map/ppermute | solution.py:499
  12.8 10.3 %collective-permute-start.11 = (bf16[656,128]{1,0:T(8,128)(2,1)S(1)}, bf16[656,128]{1,0:T(8,128)(2,1)S(1)}, u32[]{:S(2)}, u32[]{:S(2)}) collective-permute-start(bf16[656,128]{1,0:T(8,128)(2,1)S(1)} %collective-permute-done.3.rest_4_), channel_id=1, source_target_pairs={{0,1},{1,0},{2,3},{3,2},{4,5},{5,4},{6,7},{7,6},{8,24},{9,25},{10,... | collective-permute-start | bytes 503816 | tf_op jit(solution)/shard_map/ppermute | solution.py:499
  13.4 9.7 %collective-permute-start.18 = (bf16[656,128]{1,0:T(8,128)(2,1)S(1)}, bf16[656,128]{1,0:T(8,128)(2,1)S(1)}, u32[]{:S(2)}, u32[]{:S(2)}) collective-permute-start(bf16[656,128]{1,0:T(8,128)(2,1)S(1)} %collective-permute-done.2.rest_3_), channel_id=1, source_target_pairs={{0,8},{1,9},{2,10},{3,11},{4,12},{5,13},{6,14},{7,15},{8,0},{9,1},... | collective-permute-start | bytes 503816 | tf_op jit(solution)/shard_map/ppermute | solution.py:499
  19.8 9.0 %collective-permute-start.7 = (bf16[656,128]{1,0:T(8,128)(2,1)S(1)}, bf16[656,128]{1,0:T(8,128)(2,1)S(1)}, u32[]{:S(2)}, u32[]{:S(2)}) collective-permute-start(bf16[656,128]{1,0:T(8,128)(2,1)S(1)} %collective-permute-done.2.rest_3_), channel_id=1, source_target_pairs={{0,6},{1,7},{2,4},{3,5},{4,2},{5,3},{6,0},{7,1},{8,14},{9,15},{10,... | collective-permute-start | bytes 503816 | tf_op jit(solution)/shard_map/ppermute | solution.py:499
  23.1 9.3 %collective-permute-start.13 = (bf16[656,128]{1,0:T(8,128)(2,1)S(1)}, bf16[656,128]{1,0:T(8,128)(2,1)S(1)}, u32[]{:S(2)}, u32[]{:S(2)}) collective-permute-start(bf16[656,128]{1,0:T(8,128)(2,1)S(1)} %collective-permute-done.1.rest_2_), channel_id=1, source_target_pairs={{0,2},{1,3},{2,0},{3,1},{4,6},{5,7},{6,4},{7,5},{8,10},{9,11},{10,... | collective-permute-start | bytes 503816 | tf_op jit(solution)/shard_map/ppermute | solution.py:499
  23.2 9.2 %collective-permute-start.9 = (bf16[656,128]{1,0:T(8,128)(2,1)S(1)}, bf16[656,128]{1,0:T(8,128)(2,1)S(1)}, u32[]{:S(2)}, u32[]{:S(2)}) collective-permute-start(bf16[656,128]{1,0:T(8,128)(2,1)S(1)} %collective-permute-done.1.rest_2_), channel_id=1, source_target_pairs={{0,16},{1,17},{2,18},{3,19},{4,20},{5,21},{6,22},{7,23},{8,9},{9,8... | collective-permute-start | bytes 503816 | tf_op jit(solution)/shard_map/ppermute | solution.py:499
  29.9 9.1 %collective-permute-start.5 = (bf16[656,128]{1,0:T(8,128)(2,1)S(1)}, bf16[656,128]{1,0:T(8,128)(2,1)S(1)}, u32[]{:S(2)}, u32[]{:S(2)}) collective-permute-start(bf16[656,128]{1,0:T(8,128)(2,1)S(1)} %collective-permute-done.rest_1_), channel_id=1, source_target_pairs={{0,6},{1,7},{2,4},{3,5},{4,2},{5,3},{6,0},{7,1},{8,14},{9,15},{10,... | collective-permute-start | bytes 503816 | tf_op jit(solution)/shard_map/ppermute | solution.py:499
  32.4 9.7 %collective-permute-start.4 = (bf16[656,128]{1,0:T(8,128)(2,1)S(1)}, bf16[656,128]{1,0:T(8,128)(2,1)S(1)}, u32[]{:S(2)}, u32[]{:S(2)}) collective-permute-start(bf16[656,128]{1,0:T(8,128)(2,1)S(1)} %collective-permute-done.rest_1_), channel_id=1, source_target_pairs={{0,2},{1,3},{2,0},{3,1},{4,6},{5,7},{6,4},{7,5},{8,10},{9,11},{10,... | collective-permute-start | bytes 503816 | tf_op jit(solution)/shard_map/ppermute | solution.py:499
  32.5 9.7 %collective-permute-start.27 = (bf16[656,128]{1,0:T(8,128)(2,1)S(1)}, bf16[656,128]{1,0:T(8,128)(2,1)S(1)}, u32[]{:S(2)}, u32[]{:S(2)}) collective-permute-start(bf16[656,128]{1,0:T(8,128)(2,1)S(1)} %collective-permute-done.11.rest_12_), channel_id=1, source_target_pairs={{0,8},{1,9},{2,10},{3,11},{4,12},{5,13},{6,14},{7,15},{8,0},{9,1},... | collective-permute-start | bytes 503816 | tf_op jit(solution)/shard_map/ppermute | solution.py:499
  34.2 8.5 %collective-permute-start.23 = (bf16[656,128]{1,0:T(8,128)(2,1)S(1)}, bf16[656,128]{1,0:T(8,128)(2,1)S(1)}, u32[]{:S(2)}, u32[]{:S(2)}) collective-permute-start(bf16[656,128]{1,0:T(8,128)(2,1)S(1)} %collective-permute-done.7.rest_8_), channel_id=1, source_target_pairs={{0,8},{1,9},{2,10},{3,11},{4,12},{5,13},{6,14},{7,15},{8,0},{9,1},... | collective-permute-start | bytes 503816 | tf_op jit(solution)/shard_map/ppermute | solution.py:499
  34.2 8.6 %collective-permute-start.22 = (bf16[656,128]{1,0:T(8,128)(2,1)S(1)}, bf16[656,128]{1,0:T(8,128)(2,1)S(1)}, u32[]{:S(2)}, u32[]{:S(2)}) collective-permute-start(bf16[656,128]{1,0:T(8,128)(2,1)S(1)} %collective-permute-done.6.rest_7_), channel_id=1, source_target_pairs={{0,8},{1,9},{2,10},{3,11},{4,12},{5,13},{6,14},{7,15},{8,0},{9,1},... | collective-permute-start | bytes 503816 | tf_op jit(solution)/shard_map/ppermute | solution.py:499
  86.7 20.6 %collective-permute-start.31 = (bf16[4,656,128]{2,1,0:T(8,128)(2,1)}, bf16[4,656,128]{2,1,0:T(8,128)(2,1)S(1)}, u32[]{:S(2)}, u32[]{:S(2)}) collective-permute-start(bf16[4,656,128]{2,1,0:T(8,128)(2,1)} %get-tuple-element.24), channel_id=1, source_target_pairs={{0,8},{1,9},{2,10},{3,11},{4,12},{5,13},{6,14},{7,15},{8,0},{9,1},... | collective-permute-start | bytes 2015240 | tf_op jit(solution)/shard_map/ppermute | solution.py:499
  89.8 9.1 %collective-permute-start.46 = (bf16[656,128]{1,0:T(8,128)(2,1)S(1)}, bf16[656,128]{1,0:T(8,128)(2,1)S(1)}, u32[]{:S(2)}, u32[]{:S(2)}) collective-permute-start(bf16[656,128]{1,0:T(8,128)(2,1)S(1)} %get-tuple-element.45), channel_id=1, source_target_pairs={{0,6},{1,7},{2,4},{3,5},{4,2},{5,3},{6,0},{7,1},{8,14},{9,15},{10,... | collective-permute-start | bytes 503816 | tf_op jit(solution)/shard_map/ppermute | solution.py:499
  91.5 8.2 %collective-permute-start.38 = (bf16[656,128]{1,0:T(8,128)(2,1)S(1)}, bf16[656,128]{1,0:T(8,128)(2,1)S(1)}, u32[]{:S(2)}, u32[]{:S(2)}) collective-permute-start(bf16[656,128]{1,0:T(8,128)(2,1)S(1)} %get-tuple-element.46), channel_id=1, source_target_pairs={{0,16},{1,17},{2,18},{3,19},{4,20},{5,21},{6,22},{7,23},{8,9},{9,8... | collective-permute-start | bytes 503816 | tf_op jit(solution)/shard_map/ppermute | solution.py:499
  92.4 9.4 %collective-permute-start.37 = (bf16[656,128]{1,0:T(8,128)(2,1)S(1)}, bf16[656,128]{1,0:T(8,128)(2,1)S(1)}, u32[]{:S(2)}, u32[]{:S(2)}) collective-permute-start(bf16[656,128]{1,0:T(8,128)(2,1)S(1)} %get-tuple-element.47), channel_id=1, source_target_pairs={{0,2},{1,3},{2,0},{3,1},{4,6},{5,7},{6,4},{7,5},{8,10},{9,11},{10,... | collective-permute-start | bytes 503816 | tf_op jit(solution)/shard_map/ppermute | solution.py:499
  92.6 13.5 %collective-permute-start.47 = (bf16[656,128]{1,0:T(8,128)(2,1)S(1)}, bf16[656,128]{1,0:T(8,128)(2,1)S(1)}, u32[]{:S(2)}, u32[]{:S(2)}) collective-permute-start(bf16[656,128]{1,0:T(8,128)(2,1)S(1)} %get-tuple-element.40), channel_id=1, source_target_pairs={{0,2},{1,3},{2,0},{3,1},{4,6},{5,7},{6,4},{7,5},{8,10},{9,11},{10,... | collective-permute-start | bytes 503816 | tf_op jit(solution)/shard_map/ppermute | solution.py:499
  98.9 10.3 %collective-permute-start.42 = (bf16[656,128]{1,0:T(8,128)(2,1)S(1)}, bf16[656,128]{1,0:T(8,128)(2,1)S(1)}, u32[]{:S(2)}, u32[]{:S(2)}) collective-permute-start(bf16[656,128]{1,0:T(8,128)(2,1)S(1)} %fusion.21), channel_id=1, source_target_pairs={{0,16},{1,17},{2,18},{3,19},{4,20},{5,21},{6,22},{7,23},{8,9},{9,8... | collective-permute-start | bytes 503816 | tf_op jit(solution)/shard_map/ppermute | solution.py:499
  99.8 9.9 %collective-permute-start.45 = (bf16[656,128]{1,0:T(8,128)(2,1)S(1)}, bf16[656,128]{1,0:T(8,128)(2,1)S(1)}, u32[]{:S(2)}, u32[]{:S(2)}) collective-permute-start(bf16[656,128]{1,0:T(8,128)(2,1)S(1)} %get-tuple-element.39), channel_id=1, source_target_pairs={{0,6},{1,7},{2,4},{3,5},{4,2},{5,3},{6,0},{7,1},{8,14},{9,15},{10,... | collective-permute-start | bytes 503816 | tf_op jit(solution)/shard_map/ppermute | solution.py:499
  101.8 8.4 %collective-permute-start.41 = (bf16[656,128]{1,0:T(8,128)(2,1)S(1)}, bf16[656,128]{1,0:T(8,128)(2,1)S(1)}, u32[]{:S(2)}, u32[]{:S(2)}) collective-permute-start(bf16[656,128]{1,0:T(8,128)(2,1)S(1)} %get-tuple-element.41), channel_id=1, source_target_pairs={{0,1},{1,0},{2,3},{3,2},{4,5},{5,4},{6,7},{7,6},{8,24},{9,25},{10,... | collective-permute-start | bytes 503816 | tf_op jit(solution)/shard_map/ppermute | solution.py:499
  108.1 11.5 %collective-permute-start.44 = (bf16[656,128]{1,0:T(8,128)(2,1)S(1)}, bf16[656,128]{1,0:T(8,128)(2,1)S(1)}, u32[]{:S(2)}, u32[]{:S(2)}) collective-permute-start(bf16[656,128]{1,0:T(8,128)(2,1)S(1)} %get-tuple-element.49), channel_id=1, source_target_pairs={{0,1},{1,0},{2,3},{3,2},{4,5},{5,4},{6,7},{7,6},{8,24},{9,25},{10,... | collective-permute-start | bytes 503816 | tf_op jit(solution)/shard_map/ppermute | solution.py:499
  110.2 8.8 %collective-permute-start.39 = (bf16[656,128]{1,0:T(8,128)(2,1)S(1)}, bf16[656,128]{1,0:T(8,128)(2,1)S(1)}, u32[]{:S(2)}, u32[]{:S(2)}) collective-permute-start(bf16[656,128]{1,0:T(8,128)(2,1)S(1)} %get-tuple-element.44), channel_id=1, source_target_pairs={{0,1},{1,0},{2,3},{3,2},{4,5},{5,4},{6,7},{7,6},{8,24},{9,25},{10,... | collective-permute-start | bytes 503816 | tf_op jit(solution)/shard_map/ppermute | solution.py:499
  (57 other events, 500.3 us)
where the time goes:
time: 151 us
  waiting for transfers between devices  60.5 us (40%)
  starting transfers between devices  42.7 us (28%)
  Pallas kernels  35.5 us (24%)
  other arithmetic  5.75 us (4%)
  local copies, waits for them, and re-layouts  4.47 us (3%)
  between operations  1.74 us (1%)
    ppermute x50, waiting for transfers between devices, hop(): return lax.ppermute(v, ('dp', 'fsdp'), pairs)  46.2 us
    ppermute x50, starting transfers between devices, hop(): return lax.ppermute(v, ('dp', 'fsdp'), pairs)  40.3 us
    pallas_call x1, Pallas kernels, run_step(): pl.pallas_call(body, out_shape=out_shape, in_specs=[sm, sm, hb, vm, hb] +...  31.5 us
    ppermute x5, waiting for transfers between devices, local(): lax.ppermute(squares, axis, [(i, i ^ d) for i in range(size)])  14.3 us
  transfers between devices with their start and end apart: 55, of which 23 were waited for; matrix products, arithmetic and copies ran while one was open for 2% of the time, Pallas kernels for 0%

commit v1 on v0

--- a/solution.py
+++ b/solution.py
@@ -24,7 +24,7 @@
 GELU_COEF = 0.7978845608028654
 CUBIC_COEF = 0.044715
 
-VMEM_LIMIT = 52 * 1024 * 1024
+VMEM_LIMIT = 48 * 1024 * 1024
 
 
 BF = jnp.bfloat16
@@ -86,7 +86,7 @@
         normed1, inv1, mixed1, qkv, probs, heads_f, heads_h, projected,
         middle, normed2, inv2, mixed2, slope, gelu_h, mlp_out,
         mod, gmod, gcol, gmlp_h, gpre_h, gmix, cond8, gmod_h,
-        lat_ref, cot_ref, bo_ref, lg_ref, sem_lat, sem_cot, sem_bo, sem_lg, sems_in, sems_out,
+        lat_ref, cot_ref, bo_ref, lg_ref, sem_lat, sem_cot, sem_bo, sem_lg,
     ) = rest[n_in + 3 + n_out :]
     gmid, gheads, gproj_h, gqkv_h = middle, mlp_out, gmlp_h, gpre_h
     _, starts, shifts, counts, rows = shard_geometry(devices)
@@ -103,15 +103,10 @@
     copy_bo = pltpu.make_async_copy(bo_ref, bo_hbm, sem_bo)
     copy_lg = pltpu.make_async_copy(lg_ref, lg_hbm, sem_lg)
     copy_lat.start()
-    copies = []
+    copy_cot.start()
     for ref, slots in zip(pieces, slots_in):
         for j, masks in enumerate(slots):
-            src = ref if len(slots) == 1 else ref.at[j]
-            copies.append(
-                pltpu.make_async_copy(src, stage.at[owner(masks)], sems_in.at[len(copies)])
-            )
-            copies[-1].start()
-    copy_cot.start()
+            stage[owner(masks)] = ref[...] if len(slots) == 1 else ref[j]
 
     chunk = 256
 
@@ -127,8 +122,6 @@
     copy_lat.wait()
     lax.fori_loop(0, tokens // chunk, norm_one, 0)
 
-    for c in copies:
-        c.wait()
     for i in range(devices):
         g = starts[i]
         n = counts[i]
@@ -365,15 +358,11 @@
     for i in range(devices):
         g = starts[i]
         stage[i] = flat[g : g + rows, :].astype(BF)
-    copies = [copy_bo, copy_lg]
     for ref, slots in zip(outs, slots_out):
         for j, masks in enumerate(slots):
-            copies.append(
-                pltpu.make_async_copy(stage.at[owner(masks)], ref.at[j], sems_out.at[len(copies) - 2])
-            )
-            copies[-1].start()
-    for c in copies:
-        c.wait()
+            ref[j] = stage[owner(masks)]
+    copy_bo.wait()
+    copy_lg.wait()
 
 
 def run_step(
@@ -391,7 +380,7 @@
         jax.ShapeDtypeStruct((tokens, D), F32),
         jax.ShapeDtypeStruct((batch, D), F32),
     ] + [
-        jax.ShapeDtypeStruct((len(slots), rows, LANES), BF) for slots in slots_out
+        pltpu.VMEM((len(slots), rows, LANES), BF) for slots in slots_out
     ]
     V = pltpu.VMEM
     scratch = [
@@ -407,19 +396,19 @@
         V((tokens, D), BF), V((tokens, FF), BF), V((tokens, D), F32), V((8, D), F32), V((8, 6 * D), BF),
         V((tokens, D), F32), V((tokens, D), F32), V((tokens, D), F32), V((tokens, D), F32),
         pltpu.SemaphoreType.DMA, pltpu.SemaphoreType.DMA, pltpu.SemaphoreType.DMA, pltpu.SemaphoreType.DMA,
-        pltpu.SemaphoreType.DMA((devices,)), pltpu.SemaphoreType.DMA((devices,)),
     ]
     body = functools.partial(step_kernel, devices, seq, batch, slots_in, slots_out)
     res = pl.pallas_call(
         body,
         out_shape=out_shape,
-        in_specs=[sm, sm, hb, vm, hb] + [hb] * len(pieces),
-        out_specs=[hb, hb, vm] + [hb] * len(slots_out),
+        in_specs=[sm, sm, hb, vm, hb] + [vm] * len(pieces),
+        out_specs=[hb, hb, vm] + [vm] * len(slots_out),
         scratch_shapes=scratch,
         compiler_params=pltpu.CompilerParams(vmem_limit_bytes=VMEM_LIMIT),
         name="step",
     )(
-        place, validity, latents.reshape(tokens, D), condition, cotangent.reshape(tokens, D), *pieces
+        place, validity, latents.reshape(tokens, D), condition, cotangent.reshape(tokens, D),
+        *[pltpu.with_memory_space_constraint(p, pltpu.VMEM) for p in pieces],
     )
     return res[0], res[1], res[2], res[3:]
 
@@ -556,11 +545,14 @@
         )
         parts = [lax.psum_scatter(chunks, both, scatter_dimension=0, tiled=False)]
     grad, squares = unshift(shift, parts, length)
-    for axis, size in (("dp", outer), ("fsdp", inner)):
-        d = 1
-        while d < size:
-            squares = squares + lax.ppermute(squares, axis, [(i, i ^ d) for i in range(size)])
-            d *= 2
+    if (outer, inner) == (4, 8):
+        rounds = ((8,), (16, 1, 17), (2, 4, 6))
+    else:
+        rounds = tuple((1 << k,) for k in range((devices - 1).bit_length()))
+    for masks in rounds:
+        came = [lax.ppermute(squares, both, [(i, i ^ m) for i in range(devices)]) for m in masks]
+        for v in came:
+            squares = squares + v
     clip_factor = jnp.minimum(1.0, MAX_NORM / (jnp.sqrt(squares[0, 0]) + NORM_EPS))
     grad_shard = grad.reshape(-1)[:length]
     clipped = grad_shard * clip_factor

time: 151 us -> 145 us (0.960)
  waiting for transfers between devices: 60.5 us -> 48.6 us
  starting transfers between devices: 42.7 us -> 48.6 us
  local copies, waits for them, and re-layouts: 4.47 us -> 8.59 us
  Pallas kernels: 35.5 us -> 31.8 us
    ppermute x5 -> x7, waiting for transfers between devices: 14.3 us -> 5.55 us  [local(): lax.ppermute(squares, both, [(i, i ^ m) for i in range(devices)])]
    ppermute x5 -> x7, starting transfers between devices: 2.39 us -> 7.88 us  [local(): lax.ppermute(squares, both, [(i, i ^ m) for i in range(devices)])]
    unnamed x52 -> x28, local copies, waits for them, and re-layouts: 2.23 us -> 6.34 us
    pallas_call x1, Pallas kernels: 31.5 us -> 27.8 us  [run_step(): pl.pallas_call(body, out_shape=out_shape, in_specs=[sm, sm, hb, vm, hb] +...]
    ppermute x50, waiting for transfers between devices: 46.2 us -> 43.1 us  [hop(): return lax.ppermute(v, ('dp', 'fsdp'), pairs)]
  transfers between devices with their start and end apart: 55 -> 57, of which waited for: 23 -> 23; matrix products, arithmetic and copies ran while one was open for 2% -> 2% of each run, Pallas kernels for 0% -> 0%
where the time goes in v1:
time: 145 us; the launch traced here: 144 us
  starting transfers between devices  48.6 us (34%)
  waiting for transfers between devices  48.6 us (34%)
  Pallas kernels  31.8 us (22%)
  local copies, waits for them, and re-layouts  8.59 us (6%)
  other arithmetic  5.07 us (3%)
  between operations  1.57 us (1%)
    ppermute x50, waiting for transfers between devices, hop(): return lax.ppermute(v, ('dp', 'fsdp'), pairs)  43.1 us
    ppermute x50, starting transfers between devices, hop(): return lax.ppermute(v, ('dp', 'fsdp'), pairs)  40.8 us
    pallas_call x1, Pallas kernels, run_step(): pl.pallas_call(body, out_shape=out_shape, in_specs=[sm, sm, hb, vm, hb] +...  27.8 us
    ppermute x7, starting transfers between devices, local(): lax.ppermute(squares, both, [(i, i ^ m) for i in range(devices)])  7.88 us
    unnamed x28, local copies, waits for them, and re-layouts  6.34 us
    ppermute x7, waiting for transfers between devices, local(): lax.ppermute(squares, both, [(i, i ^ m) for i in range(devices)])  5.55 us
  transfers between devices with their start and end apart: 57, of which 23 were waited for; matrix products, arithmetic and copies ran while one was open for 2% of the time, Pallas kernels for 0%

profile of v1, /device:TPU:0, one launch (start us, length us, event | category | flops | bytes accessed | tf_op | source)
XLA Modules:
  0.0 144.3 jit_solution(16596480527583846275)
XLA Ops:
  0.6 1.7 %pad_bitcast_fusion.x_ref = f32[656,128]{1,0:T(8,128)} fusion(f32[83112]{0:T(1024)} %param.11), kind=kLoop, calls=%fused_computation.36 | loop fusion | bytes 668320 | tf_op jit(solution)/shard_map/reshape | solution.py:425
  2.4 1.8 %shift.1.rest_0_ = bf16[656,128]{1,0:T(8,128)(2,1)} custom-call(s32[1]{0:T(128)} %bitcast.4.s_ref, f32[656,128]{1,0:T(8,128)} %pad_bitcast_fusion.x_ref), custom_call_target="tpu_custom_call" | custom-call | tf_op jit(solution)/shard_map/shift/pallas_call | solution.py:426
  4.1 3.1 %collective-permute-start.3 = (bf16[656,128]{1,0:T(8,128)(2,1)}, bf16[656,128]{1,0:T(8,128)(2,1)S(1)}, u32[]{:S(2)}, u32[]{:S(2)}) collective-permute-start(bf16[656,128]{1,0:T(8,128)(2,1)} %shift.1.rest_0_), channel_id=1, source_target_pairs={{0,2},{1,3},{2,0},{3,1},{4,6},{5,7},{6,4},{7,5},{8,10},{9,11},{10,... | collective-permute-start | bytes 503816 | tf_op jit(solution)/shard_map/ppermute | solution.py:488
  8.7 2.6 %collective-permute-start.1 = (bf16[656,128]{1,0:T(8,128)(2,1)}, bf16[656,128]{1,0:T(8,128)(2,1)S(1)}, u32[]{:S(2)}, u32[]{:S(2)}) collective-permute-start(bf16[656,128]{1,0:T(8,128)(2,1)} %shift.1.rest_0_), channel_id=1, source_target_pairs={{0,4},{1,5},{2,6},{3,7},{4,0},{5,1},{6,2},{7,3},{8,12},{9,13},{10,... | collective-permute-start | bytes 503816 | tf_op jit(solution)/shard_map/ppermute | solution.py:488
  14.7 5.1 %collective-permute-done.1.rest_2_ = bf16[656,128]{1,0:T(8,128)(2,1)S(1)} collective-permute-done((bf16[656,128]{1,0:T(8,128)(2,1)}, bf16[656,128]{1,0:T(8,128)(2,1)S(1)}, u32[]{:S(2)}, u32[]{:S(2)}) %collective-permute-start.1) | collective-permute-done | bytes 167968 | tf_op jit(solution)/shard_map/ppermute | solution.py:488
  19.8 2.5 %collective-permute-start.7 = (bf16[656,128]{1,0:T(8,128)(2,1)S(1)}, bf16[656,128]{1,0:T(8,128)(2,1)S(1)}, u32[]{:S(2)}, u32[]{:S(2)}) collective-permute-start(bf16[656,128]{1,0:T(8,128)(2,1)S(1)} %collective-permute-done.2.rest_3_), channel_id=1, source_target_pairs={{0,6},{1,7},{2,4},{3,5},{4,2},{5,3},{6,0},{7,1},{8,14},{9,15},{10,... | collective-permute-start | bytes 503816 | tf_op jit(solution)/shard_map/ppermute | solution.py:488
  24.5 4.3 %collective-permute-done.7.rest_8_ = bf16[656,128]{1,0:T(8,128)(2,1)S(1)} collective-permute-done((bf16[656,128]{1,0:T(8,128)(2,1)S(1)}, bf16[656,128]{1,0:T(8,128)(2,1)S(1)}, u32[]{:S(2)}, u32[]{:S(2)}) %collective-permute-start.7) | collective-permute-done | bytes 167968 | tf_op jit(solution)/shard_map/ppermute | solution.py:488
  29.8 2.6 %collective-permute-start.5 = (bf16[656,128]{1,0:T(8,128)(2,1)S(1)}, bf16[656,128]{1,0:T(8,128)(2,1)S(1)}, u32[]{:S(2)}, u32[]{:S(2)}) collective-permute-start(bf16[656,128]{1,0:T(8,128)(2,1)S(1)} %collective-permute-done.rest_1_), channel_id=1, source_target_pairs={{0,6},{1,7},{2,4},{3,5},{4,2},{5,3},{6,0},{7,1},{8,14},{9,15},{10,... | collective-permute-start | bytes 503816 | tf_op jit(solution)/shard_map/ppermute | solution.py:488
  34.7 4.3 %collective-permute-done.5.rest_6_ = bf16[656,128]{1,0:T(8,128)(2,1)S(1)} collective-permute-done((bf16[656,128]{1,0:T(8,128)(2,1)S(1)}, bf16[656,128]{1,0:T(8,128)(2,1)S(1)}, u32[]{:S(2)}, u32[]{:S(2)}) %collective-permute-start.5) | collective-permute-done | bytes 167968 | tf_op jit(solution)/shard_map/ppermute | solution.py:488
  38.9 2.2 %collective-permute-start.10 = (bf16[656,128]{1,0:T(8,128)(2,1)S(1)}, bf16[656,128]{1,0:T(8,128)(2,1)S(1)}, u32[]{:S(2)}, u32[]{:S(2)}) collective-permute-start(bf16[656,128]{1,0:T(8,128)(2,1)S(1)} %collective-permute-done.6.rest_7_), channel_id=1, source_target_pairs={{0,2},{1,3},{2,0},{3,1},{4,6},{5,7},{6,4},{7,5},{8,10},{9,11},{10,... | collective-permute-start | bytes 503816 | tf_op jit(solution)/shard_map/ppermute | solution.py:488
  43.6 2.0 %collective-permute-done.10.rest_11_ = bf16[656,128]{1,0:T(8,128)(2,1)S(1)} collective-permute-done((bf16[656,128]{1,0:T(8,128)(2,1)S(1)}, bf16[656,128]{1,0:T(8,128)(2,1)S(1)}, u32[]{:S(2)}, u32[]{:S(2)}) %collective-permute-start.10) | collective-permute-done | bytes 167968 | tf_op jit(solution)/shard_map/ppermute | solution.py:488
  56.5 27.8 %step.1 = (f32[512,384]{1,0:T(8,128)}, f32[512,384]{1,0:T(8,128)}, f32[2,384]{1,0:T(2,128)}, bf16[4,656,128]{2,1,0:T(8,128)(2,1)S(1)}, bf16[4,656,128]{2,1,0:T(8...) custom-call(s32[2]{0:T(128)} %pad_add_fusion.me_ref, ...), custom_call_target="tpu_custom_call" | custom-call | tf_op jit(solution)/shard_map/step/pallas_call | solution.py:401
  89.5 2.1 %collective-permute-start.47 = (bf16[656,128]{1,0:T(8,128)(2,1)S(1)}, bf16[656,128]{1,0:T(8,128)(2,1)S(1)}, u32[]{:S(2)}, u32[]{:S(2)}) collective-permute-start(bf16[656,128]{1,0:T(8,128)(2,1)S(1)} %get-tuple-element.40), channel_id=1, source_target_pairs={{0,2},{1,3},{2,0},{3,1},{4,6},{5,7},{6,4},{7,5},{8,10},{9,11},{10,... | collective-permute-start | bytes 503816 | tf_op jit(solution)/shard_map/ppermute | solution.py:488
  91.6 4.1 %collective-permute-done.46 = bf16[656,128]{1,0:T(8,128)(2,1)S(1)} collective-permute-done((bf16[656,128]{1,0:T(8,128)(2,1)S(1)}, bf16[656,128]{1,0:T(8,128)(2,1)S(1)}, u32[]{:S(2)}, u32[]{:S(2)}) %collective-permute-start.46) | collective-permute-done | bytes 167968 | tf_op jit(solution)/shard_map/ppermute | solution.py:488
  99.6 3.4 %collective-permute-done.47 = bf16[656,128]{1,0:T(8,128)(2,1)S(1)} collective-permute-done((bf16[656,128]{1,0:T(8,128)(2,1)S(1)}, bf16[656,128]{1,0:T(8,128)(2,1)S(1)}, u32[]{:S(2)}, u32[]{:S(2)}) %collective-permute-start.47) | collective-permute-done | bytes 167968 | tf_op jit(solution)/shard_map/ppermute | solution.py:488
  107.0 1.7 %collective-permute-start.39 = (bf16[656,128]{1,0:T(8,128)(2,1)S(1)}, bf16[656,128]{1,0:T(8,128)(2,1)S(1)}, u32[]{:S(2)}, u32[]{:S(2)}) collective-permute-start(bf16[656,128]{1,0:T(8,128)(2,1)S(1)} %get-tuple-element.44), channel_id=1, source_target_pairs={{0,1},{1,0},{2,3},{3,2},{4,5},{5,4},{6,7},{7,6},{8,24},{9,25},{10,... | collective-permute-start | bytes 503816 | tf_op jit(solution)/shard_map/ppermute | solution.py:488
  110.2 2.8 %collective-permute-done.34 = bf16[656,128]{1,0:T(8,128)(2,1)S(1)} collective-permute-done((bf16[656,128]{1,0:T(8,128)(2,1)S(1)}, bf16[656,128]{1,0:T(8,128)(2,1)S(1)}, u32[]{:S(2)}, u32[]{:S(2)}) %collective-permute-start.34) | collective-permute-done | bytes 167968 | tf_op jit(solution)/shard_map/ppermute | solution.py:488
  113.0 2.8 %collective-permute-done.39 = bf16[656,128]{1,0:T(8,128)(2,1)S(1)} collective-permute-done((bf16[656,128]{1,0:T(8,128)(2,1)S(1)}, bf16[656,128]{1,0:T(8,128)(2,1)S(1)}, u32[]{:S(2)}, u32[]{:S(2)}) %collective-permute-start.39) | collective-permute-done | bytes 167968 | tf_op jit(solution)/shard_map/ppermute | solution.py:488
  116.5 3.4 %collective-permute-done.43.refs_2_ = bf16[656,128]{1,0:T(8,128)(2,1)S(1)} collective-permute-done((bf16[656,128]{1,0:T(8,128)(2,1)S(1)}, bf16[656,128]{1,0:T(8,128)(2,1)S(1)}, u32[]{:S(2)}, u32[]{:S(2)}) %collective-permute-start.43) | collective-permute-done | bytes 167968 | tf_op jit(solution)/shard_map/ppermute | solution.py:488
  119.9 3.9 %collective-permute-done.40.refs_1_ = bf16[656,128]{1,0:T(8,128)(2,1)S(1)} collective-permute-done((bf16[656,128]{1,0:T(8,128)(2,1)S(1)}, bf16[656,128]{1,0:T(8,128)(2,1)S(1)}, u32[]{:S(2)}, u32[]{:S(2)}) %collective-permute-start.40) | collective-permute-done | bytes 167968 | tf_op jit(solution)/shard_map/ppermute | solution.py:488
  124.5 2.3 %unshift.1 = (f32[656,128]{1,0:T(8,128)}, f32[8,128]{1,0:T(8,128)}) custom-call(s32[1]{0:T(128)} %bitcast.4.s_ref, bf16[656,128]{1,0:T(8,128)(2,1)} %get-tuple-element.50.refs_0_, bf16[656,128]{1,0:T(8,128)(2,1)} %copy-done.13, bf16[656,128]{1,0:T(8,128)(2,1)} %copy-done.12, bf16[656,128]{1,0:T(8,128)(2,1)} %copy-done.10, bf16[656,128]{1,0:T(8,128)(2,1)} %copy-done.11), custom_call_target="tpu_custom_call" | custom-call | tf_op jit(solution)/shard_map/unshift/pallas_call | solution.py:455
  134.6 1.8 %collective-permute-start.56 = (f32[8,128]{1,0:T(8,128)S(1)}, f32[8,128]{1,0:T(8,128)S(1)}, u32[]{:S(2)}, u32[]{:S(2)}) collective-permute-start(f32[8,128]{1,0:T(8,128)S(1)} %add_add_fusion.1), channel_id=1, source_target_pairs={{0,6},{1,7},{2,4},{3,5},{4,2},{5,3},{6,0},{7,1},{8,14},{9,15},{10,... | collective-permute-start | bytes 12296 | tf_op jit(solution)/shard_map/ppermute | solution.py:553
  136.4 2.6 %collective-permute-start.54 = (f32[8,128]{1,0:T(8,128)S(1)}, f32[8,128]{1,0:T(8,128)S(1)}, u32[]{:S(2)}, u32[]{:S(2)}) collective-permute-start(f32[8,128]{1,0:T(8,128)S(1)} %add_add_fusion.1), channel_id=1, source_target_pairs={{0,2},{1,3},{2,0},{3,1},{4,6},{5,7},{6,4},{7,5},{8,10},{9,11},{10,... | collective-permute-start | bytes 12296 | tf_op jit(solution)/shard_map/ppermute | solution.py:553
  142.2 2.1 %multiply_subtract_fusion = (f32[83112]{0:T(1024)}, f32[83112]{0:T(1024)}, f32[83112]{0:T(1024)}, f32[83112]{0:T(1024)}) fusion(f32[83112]{0:T(1024)S(1)} %copy-done.7, f32[]{:T(128)} %bitcast.25, f32[83112]{0:T(1024)S(1)} %copy-done.8, f32[83112]{0:T(1024)S(1)} %copy-done.9, f32[83968]{0:T(1024)} %bitcast.60), kind=kLoop, calls=%fused_computation.18 | loop fusion | flops 1329792 | bytes 2659588 | tf_op jit(solution)/shard_map/sub | solution.py:563
  (135 shorter events, 49.9 us)
Async XLA Ops:
  4.1 8.7 %collective-permute-start.3 = (bf16[656,128]{1,0:T(8,128)(2,1)}, bf16[656,128]{1,0:T(8,128)(2,1)S(1)}, u32[]{:S(2)}, u32[]{:S(2)}) collective-permute-start(bf16[656,128]{1,0:T(8,128)(2,1)} %shift.1.rest_0_), channel_id=1, source_target_pairs={{0,2},{1,3},{2,0},{3,1},{4,6},{5,7},{6,4},{7,5},{8,10},{9,11},{10,... | collective-permute-start | bytes 503816 | tf_op jit(solution)/shard_map/ppermute | solution.py:488
  8.7 11.1 %collective-permute-start.1 = (bf16[656,128]{1,0:T(8,128)(2,1)}, bf16[656,128]{1,0:T(8,128)(2,1)S(1)}, u32[]{:S(2)}, u32[]{:S(2)}) collective-permute-start(bf16[656,128]{1,0:T(8,128)(2,1)} %shift.1.rest_0_), channel_id=1, source_target_pairs={{0,4},{1,5},{2,6},{3,7},{4,0},{5,1},{6,2},{7,3},{8,12},{9,13},{10,... | collective-permute-start | bytes 503816 | tf_op jit(solution)/shard_map/ppermute | solution.py:488
  11.3 11.0 %collective-permute-start = (bf16[656,128]{1,0:T(8,128)(2,1)}, bf16[656,128]{1,0:T(8,128)(2,1)S(1)}, u32[]{:S(2)}, u32[]{:S(2)}) collective-permute-start(bf16[656,128]{1,0:T(8,128)(2,1)} %shift.1.rest_0_), channel_id=1, source_target_pairs={{0,16},{1,17},{2,18},{3,19},{4,20},{5,21},{6,22},{7,23},{8,9},{9,8... | collective-permute-start | bytes 503816 | tf_op jit(solution)/shard_map/ppermute | solution.py:488
  12.8 10.3 %collective-permute-start.19 = (bf16[656,128]{1,0:T(8,128)(2,1)S(1)}, bf16[656,128]{1,0:T(8,128)(2,1)S(1)}, u32[]{:S(2)}, u32[]{:S(2)}) collective-permute-start(bf16[656,128]{1,0:T(8,128)(2,1)S(1)} %collective-permute-done.3.rest_4_), channel_id=1, source_target_pairs={{0,8},{1,9},{2,10},{3,11},{4,12},{5,13},{6,14},{7,15},{8,0},{9,1},... | collective-permute-start | bytes 503816 | tf_op jit(solution)/shard_map/ppermute | solution.py:488
  12.8 10.3 %collective-permute-start.11 = (bf16[656,128]{1,0:T(8,128)(2,1)S(1)}, bf16[656,128]{1,0:T(8,128)(2,1)S(1)}, u32[]{:S(2)}, u32[]{:S(2)}) collective-permute-start(bf16[656,128]{1,0:T(8,128)(2,1)S(1)} %collective-permute-done.3.rest_4_), channel_id=1, source_target_pairs={{0,1},{1,0},{2,3},{3,2},{4,5},{5,4},{6,7},{7,6},{8,24},{9,25},{10,... | collective-permute-start | bytes 503816 | tf_op jit(solution)/shard_map/ppermute | solution.py:488
  13.4 9.8 %collective-permute-start.18 = (bf16[656,128]{1,0:T(8,128)(2,1)S(1)}, bf16[656,128]{1,0:T(8,128)(2,1)S(1)}, u32[]{:S(2)}, u32[]{:S(2)}) collective-permute-start(bf16[656,128]{1,0:T(8,128)(2,1)S(1)} %collective-permute-done.2.rest_3_), channel_id=1, source_target_pairs={{0,8},{1,9},{2,10},{3,11},{4,12},{5,13},{6,14},{7,15},{8,0},{9,1},... | collective-permute-start | bytes 503816 | tf_op jit(solution)/shard_map/ppermute | solution.py:488
  19.8 9.0 %collective-permute-start.7 = (bf16[656,128]{1,0:T(8,128)(2,1)S(1)}, bf16[656,128]{1,0:T(8,128)(2,1)S(1)}, u32[]{:S(2)}, u32[]{:S(2)}) collective-permute-start(bf16[656,128]{1,0:T(8,128)(2,1)S(1)} %collective-permute-done.2.rest_3_), channel_id=1, source_target_pairs={{0,6},{1,7},{2,4},{3,5},{4,2},{5,3},{6,0},{7,1},{8,14},{9,15},{10,... | collective-permute-start | bytes 503816 | tf_op jit(solution)/shard_map/ppermute | solution.py:488
  23.1 9.3 %collective-permute-start.13 = (bf16[656,128]{1,0:T(8,128)(2,1)S(1)}, bf16[656,128]{1,0:T(8,128)(2,1)S(1)}, u32[]{:S(2)}, u32[]{:S(2)}) collective-permute-start(bf16[656,128]{1,0:T(8,128)(2,1)S(1)} %collective-permute-done.1.rest_2_), channel_id=1, source_target_pairs={{0,2},{1,3},{2,0},{3,1},{4,6},{5,7},{6,4},{7,5},{8,10},{9,11},{10,... | collective-permute-start | bytes 503816 | tf_op jit(solution)/shard_map/ppermute | solution.py:488
  23.2 9.2 %collective-permute-start.9 = (bf16[656,128]{1,0:T(8,128)(2,1)S(1)}, bf16[656,128]{1,0:T(8,128)(2,1)S(1)}, u32[]{:S(2)}, u32[]{:S(2)}) collective-permute-start(bf16[656,128]{1,0:T(8,128)(2,1)S(1)} %collective-permute-done.1.rest_2_), channel_id=1, source_target_pairs={{0,16},{1,17},{2,18},{3,19},{4,20},{5,21},{6,22},{7,23},{8,9},{9,8... | collective-permute-start | bytes 503816 | tf_op jit(solution)/shard_map/ppermute | solution.py:488
  29.8 9.1 %collective-permute-start.5 = (bf16[656,128]{1,0:T(8,128)(2,1)S(1)}, bf16[656,128]{1,0:T(8,128)(2,1)S(1)}, u32[]{:S(2)}, u32[]{:S(2)}) collective-permute-start(bf16[656,128]{1,0:T(8,128)(2,1)S(1)} %collective-permute-done.rest_1_), channel_id=1, source_target_pairs={{0,6},{1,7},{2,4},{3,5},{4,2},{5,3},{6,0},{7,1},{8,14},{9,15},{10,... | collective-permute-start | bytes 503816 | tf_op jit(solution)/shard_map/ppermute | solution.py:488
  32.4 9.7 %collective-permute-start.4 = (bf16[656,128]{1,0:T(8,128)(2,1)S(1)}, bf16[656,128]{1,0:T(8,128)(2,1)S(1)}, u32[]{:S(2)}, u32[]{:S(2)}) collective-permute-start(bf16[656,128]{1,0:T(8,128)(2,1)S(1)} %collective-permute-done.rest_1_), channel_id=1, source_target_pairs={{0,2},{1,3},{2,0},{3,1},{4,6},{5,7},{6,4},{7,5},{8,10},{9,11},{10,... | collective-permute-start | bytes 503816 | tf_op jit(solution)/shard_map/ppermute | solution.py:488
  32.4 9.7 %collective-permute-start.27 = (bf16[656,128]{1,0:T(8,128)(2,1)S(1)}, bf16[656,128]{1,0:T(8,128)(2,1)S(1)}, u32[]{:S(2)}, u32[]{:S(2)}) collective-permute-start(bf16[656,128]{1,0:T(8,128)(2,1)S(1)} %collective-permute-done.11.rest_12_), channel_id=1, source_target_pairs={{0,8},{1,9},{2,10},{3,11},{4,12},{5,13},{6,14},{7,15},{8,0},{9,1},... | collective-permute-start | bytes 503816 | tf_op jit(solution)/shard_map/ppermute | solution.py:488
  34.2 8.5 %collective-permute-start.23 = (bf16[656,128]{1,0:T(8,128)(2,1)S(1)}, bf16[656,128]{1,0:T(8,128)(2,1)S(1)}, u32[]{:S(2)}, u32[]{:S(2)}) collective-permute-start(bf16[656,128]{1,0:T(8,128)(2,1)S(1)} %collective-permute-done.7.rest_8_), channel_id=1, source_target_pairs={{0,8},{1,9},{2,10},{3,11},{4,12},{5,13},{6,14},{7,15},{8,0},{9,1},... | collective-permute-start | bytes 503816 | tf_op jit(solution)/shard_map/ppermute | solution.py:488
  34.2 8.5 %collective-permute-start.22 = (bf16[656,128]{1,0:T(8,128)(2,1)S(1)}, bf16[656,128]{1,0:T(8,128)(2,1)S(1)}, u32[]{:S(2)}, u32[]{:S(2)}) collective-permute-start(bf16[656,128]{1,0:T(8,128)(2,1)S(1)} %collective-permute-done.6.rest_7_), channel_id=1, source_target_pairs={{0,8},{1,9},{2,10},{3,11},{4,12},{5,13},{6,14},{7,15},{8,0},{9,1},... | collective-permute-start | bytes 503816 | tf_op jit(solution)/shard_map/ppermute | solution.py:488
  85.0 19.2 %collective-permute-start.31 = (bf16[4,656,128]{2,1,0:T(8,128)(2,1)S(1)}, bf16[4,656,128]{2,1,0:T(8,128)(2,1)S(1)}, u32[]{:S(2)}, u32[]{:S(2)}) collective-permute-start(bf16[4,656,128]{2,1,0:T(8,128)(2,1)S(1)} %get-tuple-element.24), channel_id=1, source_target_pairs={{0,8},{1,9},{2,10},{3,11},{4,12},{5,13},{6,14},{7,15},{8,0},{9,1},... | collective-permute-start | bytes 2015240 | tf_op jit(solution)/shard_map/ppermute | solution.py:488
  86.7 9.1 %collective-permute-start.46 = (bf16[656,128]{1,0:T(8,128)(2,1)S(1)}, bf16[656,128]{1,0:T(8,128)(2,1)S(1)}, u32[]{:S(2)}, u32[]{:S(2)}) collective-permute-start(bf16[656,128]{1,0:T(8,128)(2,1)S(1)} %get-tuple-element.45), channel_id=1, source_target_pairs={{0,6},{1,7},{2,4},{3,5},{4,2},{5,3},{6,0},{7,1},{8,14},{9,15},{10,... | collective-permute-start | bytes 503816 | tf_op jit(solution)/shard_map/ppermute | solution.py:488
  88.4 8.3 %collective-permute-start.38 = (bf16[656,128]{1,0:T(8,128)(2,1)S(1)}, bf16[656,128]{1,0:T(8,128)(2,1)S(1)}, u32[]{:S(2)}, u32[]{:S(2)}) collective-permute-start(bf16[656,128]{1,0:T(8,128)(2,1)S(1)} %get-tuple-element.46), channel_id=1, source_target_pairs={{0,16},{1,17},{2,18},{3,19},{4,20},{5,21},{6,22},{7,23},{8,9},{9,8... | collective-permute-start | bytes 503816 | tf_op jit(solution)/shard_map/ppermute | solution.py:488
  89.3 9.4 %collective-permute-start.37 = (bf16[656,128]{1,0:T(8,128)(2,1)S(1)}, bf16[656,128]{1,0:T(8,128)(2,1)S(1)}, u32[]{:S(2)}, u32[]{:S(2)}) collective-permute-start(bf16[656,128]{1,0:T(8,128)(2,1)S(1)} %get-tuple-element.47), channel_id=1, source_target_pairs={{0,2},{1,3},{2,0},{3,1},{4,6},{5,7},{6,4},{7,5},{8,10},{9,11},{10,... | collective-permute-start | bytes 503816 | tf_op jit(solution)/shard_map/ppermute | solution.py:488
  89.5 13.5 %collective-permute-start.47 = (bf16[656,128]{1,0:T(8,128)(2,1)S(1)}, bf16[656,128]{1,0:T(8,128)(2,1)S(1)}, u32[]{:S(2)}, u32[]{:S(2)}) collective-permute-start(bf16[656,128]{1,0:T(8,128)(2,1)S(1)} %get-tuple-element.40), channel_id=1, source_target_pairs={{0,2},{1,3},{2,0},{3,1},{4,6},{5,7},{6,4},{7,5},{8,10},{9,11},{10,... | collective-permute-start | bytes 503816 | tf_op jit(solution)/shard_map/ppermute | solution.py:488
  95.7 10.3 %collective-permute-start.42 = (bf16[656,128]{1,0:T(8,128)(2,1)S(1)}, bf16[656,128]{1,0:T(8,128)(2,1)S(1)}, u32[]{:S(2)}, u32[]{:S(2)}) collective-permute-start(bf16[656,128]{1,0:T(8,128)(2,1)S(1)} %fusion.21), channel_id=1, source_target_pairs={{0,16},{1,17},{2,18},{3,19},{4,20},{5,21},{6,22},{7,23},{8,9},{9,8... | collective-permute-start | bytes 503816 | tf_op jit(solution)/shard_map/ppermute | solution.py:488
  96.6 10.0 %collective-permute-start.45 = (bf16[656,128]{1,0:T(8,128)(2,1)S(1)}, bf16[656,128]{1,0:T(8,128)(2,1)S(1)}, u32[]{:S(2)}, u32[]{:S(2)}) collective-permute-start(bf16[656,128]{1,0:T(8,128)(2,1)S(1)} %get-tuple-element.39), channel_id=1, source_target_pairs={{0,6},{1,7},{2,4},{3,5},{4,2},{5,3},{6,0},{7,1},{8,14},{9,15},{10,... | collective-permute-start | bytes 503816 | tf_op jit(solution)/shard_map/ppermute | solution.py:488
  98.7 8.3 %collective-permute-start.41 = (bf16[656,128]{1,0:T(8,128)(2,1)S(1)}, bf16[656,128]{1,0:T(8,128)(2,1)S(1)}, u32[]{:S(2)}, u32[]{:S(2)}) collective-permute-start(bf16[656,128]{1,0:T(8,128)(2,1)S(1)} %get-tuple-element.41), channel_id=1, source_target_pairs={{0,1},{1,0},{2,3},{3,2},{4,5},{5,4},{6,7},{7,6},{8,24},{9,25},{10,... | collective-permute-start | bytes 503816 | tf_op jit(solution)/shard_map/ppermute | solution.py:488
  105.0 11.5 %collective-permute-start.44 = (bf16[656,128]{1,0:T(8,128)(2,1)S(1)}, bf16[656,128]{1,0:T(8,128)(2,1)S(1)}, u32[]{:S(2)}, u32[]{:S(2)}) collective-permute-start(bf16[656,128]{1,0:T(8,128)(2,1)S(1)} %get-tuple-element.49), channel_id=1, source_target_pairs={{0,1},{1,0},{2,3},{3,2},{4,5},{5,4},{6,7},{7,6},{8,24},{9,25},{10,... | collective-permute-start | bytes 503816 | tf_op jit(solution)/shard_map/ppermute | solution.py:488
  107.0 8.8 %collective-permute-start.39 = (bf16[656,128]{1,0:T(8,128)(2,1)S(1)}, bf16[656,128]{1,0:T(8,128)(2,1)S(1)}, u32[]{:S(2)}, u32[]{:S(2)}) collective-permute-start(bf16[656,128]{1,0:T(8,128)(2,1)S(1)} %get-tuple-element.44), channel_id=1, source_target_pairs={{0,1},{1,0},{2,3},{3,2},{4,5},{5,4},{6,7},{7,6},{8,24},{9,25},{10,... | collective-permute-start | bytes 503816 | tf_op jit(solution)/shard_map/ppermute | solution.py:488
  (47 other events, 251.7 us)

commit v2 on v1

--- a/solution.py
+++ b/solution.py
@@ -425,11 +425,11 @@
     padded = jnp.pad(params, (0, rows * LANES - params.shape[0])).reshape(rows, LANES)
     return pl.pallas_call(
         shift_kernel,
-        out_shape=jax.ShapeDtypeStruct((rows, LANES), BF),
+        out_shape=pltpu.VMEM((rows, LANES), BF),
         in_specs=[pl.BlockSpec(memory_space=pltpu.SMEM), pl.BlockSpec(memory_space=pltpu.VMEM)],
         out_specs=pl.BlockSpec(memory_space=pltpu.VMEM),
         name="shift",
-    )(shift, padded)
+    )(shift, pltpu.with_memory_space_constraint(padded, pltpu.VMEM))
 
 
 def unshift_kernel(length, n, s_ref, *refs):
@@ -454,22 +454,48 @@
     rows = parts[0].shape[0]
     return pl.pallas_call(
         functools.partial(unshift_kernel, length, len(parts)),
-        out_shape=[jax.ShapeDtypeStruct((rows, LANES), F32), jax.ShapeDtypeStruct((8, LANES), F32)],
+        out_shape=[pltpu.VMEM((rows, LANES), F32), pltpu.VMEM((8, LANES), F32)],
         in_specs=[pl.BlockSpec(memory_space=pltpu.SMEM)]
         + [pl.BlockSpec(memory_space=pltpu.VMEM)] * len(parts),
         out_specs=[pl.BlockSpec(memory_space=pltpu.VMEM)] * 2,
         name="unshift",
-    )(shift, *parts)
+    )(shift, *[pltpu.with_memory_space_constraint(p, pltpu.VMEM) for p in parts])
 
 
 HOPS = {"a": 16, "b": 1, "z1": 2, "z2": 4, "z3": 6}
 GATHER = (
-    (16, "a"), (4, "z2"), (1, "b"), (2, "z1"), (18, "z1"), (22, "z3"), (17, "a"), (7, "z3"),
-    (5, "b"), (20, "a"), (19, "z1"), (3, "b"), (21, "a"), (6, "z1"), (23, "b"),
+    (2, "z1"),
+    (6, "z3"),
+    (1, "b"),
+    (16, "a"),
+    (3, "b"),
+    (18, "a"),
+    (5, "z2"),
+    (17, "a"),
+    (22, "a"),
+    (4, "z1"),
+    (19, "a"),
+    (7, "b"),
+    (23, "b"),
+    (20, "z1"),
+    (21, "a"),
 )
 SCATTER = (
-    (23, "z3"), (20, "a"), (7, "z1"), (21, "a"), (3, "b"), (19, "z1"), (6, "z1"), (22, "z3"),
-    (5, "b"), (18, "a"), (17, "b"), (4, "z2"), (2, "z1"), (1, "b"), (16, "a"),
+    (23, "z1"),
+    (7, "b"),
+    (5, "b"),
+    (22, "z1"),
+    (19, "b"),
+    (21, "b"),
+    (6, "z1"),
+    (3, "b"),
+    (20, "a"),
+    (18, "a"),
+    (17, "b"),
+    (4, "z2"),
+    (2, "z1"),
+    (1, "b"),
+    (16, "a"),
 )
 GATHER_NODES = (0,) + tuple(n for n, _ in GATHER)
 SCATTER_NODES = tuple(n for n, _ in SCATTER) + (0,)
@@ -507,7 +533,7 @@
     own = shift_shard(shift, params, rows)
     if (outer, inner) == (4, 8):
         core = jnp.bitwise_and(jnp.right_shift(me, 3), 1)
-        place = jnp.stack([me, core])
+        own, place = lax.optimization_barrier((own, jnp.stack([me, core])))
         got = {0: own}
         for node, kind in GATHER:
             got[node] = hop(got[node ^ HOPS[kind]], kind)
@@ -549,12 +575,12 @@
         rounds = ((8,), (16, 1, 17), (2, 4, 6))
     else:
         rounds = tuple((1 << k,) for k in range((devices - 1).bit_length()))
+    grad_shard = grad.reshape(-1)[:length]
     for masks in rounds:
         came = [lax.ppermute(squares, both, [(i, i ^ m) for i in range(devices)]) for m in masks]
         for v in came:
             squares = squares + v
     clip_factor = jnp.minimum(1.0, MAX_NORM / (jnp.sqrt(squares[0, 0]) + NORM_EPS))
-    grad_shard = grad.reshape(-1)[:length]
     clipped = grad_shard * clip_factor
     new_one = BETA_ONE * moment_one + (1.0 - BETA_ONE) * clipped
     new_two = BETA_TWO * moment_two + (1.0 - BETA_TWO) * clipped * clipped

time: 145 us -> 129 us (0.89)
  local copies, waits for them, and re-layouts: 8.59 us -> 1.53 us
  Pallas kernels: 31.8 us -> 27.8 us
  other arithmetic: 5.07 us -> 2.76 us
    unnamed x28 -> x6, local copies, waits for them, and re-layouts: 6.34 us -> 0.01 us
    pallas_call x1, Pallas kernels: 2.25 us -> 0.33 us  [unshift(): pl.pallas_call(functools.partial(unshift_kernel, length, len(parts)), out...]
    pallas_call x1, Pallas kernels: 1.76 us -> 0.12 us  [shift_shard(): pl.pallas_call(shift_kernel, out_shape=pltpu.VMEM((rows, LANES), BF), in_...]
  transfers between devices with their start and end apart: 57 -> 57, of which waited for: 23 -> 25; matrix products, arithmetic and copies ran while one was open for 2% -> 1% of each run, Pallas kernels for 0% -> 0%
where the time goes in v2:
time: 129 us
  waiting for transfers between devices  47.6 us (37%)
  starting transfers between devices  47.4 us (37%)
  Pallas kernels  27.8 us (22%)
  other arithmetic  2.76 us (2%)
  between operations  1.55 us (1%)
  local copies, waits for them, and re-layouts  1.53 us (1%)
    ppermute x50, waiting for transfers between devices, hop(): return lax.ppermute(v, ('dp', 'fsdp'), pairs)  41.6 us
    ppermute x50, starting transfers between devices, hop(): return lax.ppermute(v, ('dp', 'fsdp'), pairs)  39.4 us
    pallas_call x1, Pallas kernels, run_step(): pl.pallas_call(body, out_shape=out_shape, in_specs=[sm, sm, hb, vm, hb] +...  27.3 us
    ppermute x7, starting transfers between devices, local(): lax.ppermute(squares, both, [(i, i ^ m) for i in range(devices)])  7.95 us
    ppermute x7, waiting for transfers between devices, local(): lax.ppermute(squares, both, [(i, i ^ m) for i in range(devices)])  6.01 us
  transfers between devices with their start and end apart: 57, of which 25 were waited for; matrix products, arithmetic and copies ran while one was open for 1% of the time, Pallas kernels for 0%

profile of v2, /device:TPU:0, one launch (start us, length us, event | category | flops | bytes accessed | tf_op | source)
XLA Modules:
  0.0 128.6 jit_solution(14983275587300352322)
XLA Ops:
  2.4 3.0 %collective-permute-start.3 = (bf16[656,128]{1,0:T(8,128)(2,1)S(1)}, bf16[656,128]{1,0:T(8,128)(2,1)S(1)}, u32[]{:S(2)}, u32[]{:S(2)}) collective-permute-start(bf16[656,128]{1,0:T(8,128)(2,1)S(1)} %shift.1.rest_0_), channel_id=1, source_target_pairs={{0,16},{1,17},{2,18},{3,19},{4,20},{5,21},{6,22},{7,23},{8,9},{9,8... | collective-permute-start | bytes 503816 | tf_op jit(solution)/shard_map/ppermute | solution.py:514
  6.9 3.6 %collective-permute-start.1 = (bf16[656,128]{1,0:T(8,128)(2,1)S(1)}, bf16[656,128]{1,0:T(8,128)(2,1)S(1)}, u32[]{:S(2)}, u32[]{:S(2)}) collective-permute-start(bf16[656,128]{1,0:T(8,128)(2,1)S(1)} %shift.1.rest_0_), channel_id=1, source_target_pairs={{0,6},{1,7},{2,4},{3,5},{4,2},{5,3},{6,0},{7,1},{8,14},{9,15},{10,... | collective-permute-start | bytes 503816 | tf_op jit(solution)/shard_map/ppermute | solution.py:514
  11.1 1.9 %collective-permute-start.7 = (bf16[656,128]{1,0:T(8,128)(2,1)S(1)}, bf16[656,128]{1,0:T(8,128)(2,1)S(1)}, u32[]{:S(2)}, u32[]{:S(2)}) collective-permute-start(bf16[656,128]{1,0:T(8,128)(2,1)S(1)} %collective-permute-done.2.rest_3_), channel_id=1, source_target_pairs={{0,16},{1,17},{2,18},{3,19},{4,20},{5,21},{6,22},{7,23},{8,9},{9,8... | collective-permute-start | bytes 503816 | tf_op jit(solution)/shard_map/ppermute | solution.py:514
  13.0 3.0 %collective-permute-done.1.rest_2_ = bf16[656,128]{1,0:T(8,128)(2,1)S(1)} collective-permute-done((bf16[656,128]{1,0:T(8,128)(2,1)S(1)}, bf16[656,128]{1,0:T(8,128)(2,1)S(1)}, u32[]{:S(2)}, u32[]{:S(2)}) %collective-permute-start.1) | collective-permute-done | bytes 167968 | tf_op jit(solution)/shard_map/ppermute | solution.py:514
  15.9 3.9 %collective-permute-start.6 = (bf16[656,128]{1,0:T(8,128)(2,1)S(1)}, bf16[656,128]{1,0:T(8,128)(2,1)S(1)}, u32[]{:S(2)}, u32[]{:S(2)}) collective-permute-start(bf16[656,128]{1,0:T(8,128)(2,1)S(1)} %collective-permute-done.2.rest_3_), channel_id=1, source_target_pairs={{0,4},{1,5},{2,6},{3,7},{4,0},{5,1},{6,2},{7,3},{8,12},{9,13},{10,... | collective-permute-start | bytes 503816 | tf_op jit(solution)/shard_map/ppermute | solution.py:514
  21.9 5.7 %collective-permute-done.6.rest_7_ = bf16[656,128]{1,0:T(8,128)(2,1)S(1)} collective-permute-done((bf16[656,128]{1,0:T(8,128)(2,1)S(1)}, bf16[656,128]{1,0:T(8,128)(2,1)S(1)}, u32[]{:S(2)}, u32[]{:S(2)}) %collective-permute-start.6) | collective-permute-done | bytes 167968 | tf_op jit(solution)/shard_map/ppermute | solution.py:514
  30.9 3.6 %collective-permute-done.5.rest_6_ = bf16[656,128]{1,0:T(8,128)(2,1)S(1)} collective-permute-done((bf16[656,128]{1,0:T(8,128)(2,1)S(1)}, bf16[656,128]{1,0:T(8,128)(2,1)S(1)}, u32[]{:S(2)}, u32[]{:S(2)}) %collective-permute-start.5) | collective-permute-done | bytes 167968 | tf_op jit(solution)/shard_map/ppermute | solution.py:514
  38.6 3.5 %collective-permute-done.13.rest_14_ = bf16[656,128]{1,0:T(8,128)(2,1)S(1)} collective-permute-done((bf16[656,128]{1,0:T(8,128)(2,1)S(1)}, bf16[656,128]{1,0:T(8,128)(2,1)S(1)}, u32[]{:S(2)}, u32[]{:S(2)}) %collective-permute-start.13) | collective-permute-done | bytes 167968 | tf_op jit(solution)/shard_map/ppermute | solution.py:514
  45.1 27.3 %step.1 = (f32[512,384]{1,0:T(8,128)}, f32[512,384]{1,0:T(8,128)}, f32[2,384]{1,0:T(2,128)}, bf16[4,656,128]{2,1,0:T(8,128)(2,1)S(1)}, bf16[4,656,128]{2,1,0:T(8...) custom-call(s32[2]{0:T(128)} %pad_add_fusion.me_ref, ...), custom_call_target="tpu_custom_call" | custom-call | tf_op jit(solution)/shard_map/step/pallas_call | solution.py:401
  74.8 1.8 %collective-permute-start.39 = (bf16[656,128]{1,0:T(8,128)(2,1)S(1)}, bf16[656,128]{1,0:T(8,128)(2,1)S(1)}, u32[]{:S(2)}, u32[]{:S(2)}) collective-permute-start(bf16[656,128]{1,0:T(8,128)(2,1)S(1)} %get-tuple-element.50), channel_id=1, source_target_pairs={{0,2},{1,3},{2,0},{3,1},{4,6},{5,7},{6,4},{7,5},{8,10},{9,11},{10,... | collective-permute-start | bytes 503816 | tf_op jit(solution)/shard_map/ppermute | solution.py:514
  77.2 4.8 %collective-permute-done.39 = bf16[656,128]{1,0:T(8,128)(2,1)S(1)} collective-permute-done((bf16[656,128]{1,0:T(8,128)(2,1)S(1)}, bf16[656,128]{1,0:T(8,128)(2,1)S(1)}, u32[]{:S(2)}, u32[]{:S(2)}) %collective-permute-start.39) | collective-permute-done | bytes 167968 | tf_op jit(solution)/shard_map/ppermute | solution.py:514
  82.5 1.9 %collective-permute-start.40 = (bf16[656,128]{1,0:T(8,128)(2,1)S(1)}, bf16[656,128]{1,0:T(8,128)(2,1)S(1)}, u32[]{:S(2)}, u32[]{:S(2)}) collective-permute-start(bf16[656,128]{1,0:T(8,128)(2,1)S(1)} %get-tuple-element.54), channel_id=1, source_target_pairs={{0,1},{1,0},{2,3},{3,2},{4,5},{5,4},{6,7},{7,6},{8,24},{9,25},{10,... | collective-permute-start | bytes 503816 | tf_op jit(solution)/shard_map/ppermute | solution.py:514
  85.0 1.5 %collective-permute-start.43 = (bf16[656,128]{1,0:T(8,128)(2,1)S(1)}, bf16[656,128]{1,0:T(8,128)(2,1)S(1)}, u32[]{:S(2)}, u32[]{:S(2)}) collective-permute-start(bf16[656,128]{1,0:T(8,128)(2,1)S(1)} %get-tuple-element.45), channel_id=1, source_target_pairs={{0,1},{1,0},{2,3},{3,2},{4,5},{5,4},{6,7},{7,6},{8,24},{9,25},{10,... | collective-permute-start | bytes 503816 | tf_op jit(solution)/shard_map/ppermute | solution.py:514
  87.4 1.8 %collective-permute-done.40 = bf16[656,128]{1,0:T(8,128)(2,1)S(1)} collective-permute-done((bf16[656,128]{1,0:T(8,128)(2,1)S(1)}, bf16[656,128]{1,0:T(8,128)(2,1)S(1)}, u32[]{:S(2)}, u32[]{:S(2)}) %collective-permute-start.40) | collective-permute-done | bytes 167968 | tf_op jit(solution)/shard_map/ppermute | solution.py:514
  90.8 1.6 %collective-permute-start.34 = (bf16[656,128]{1,0:T(8,128)(2,1)S(1)}, bf16[656,128]{1,0:T(8,128)(2,1)S(1)}, u32[]{:S(2)}, u32[]{:S(2)}) collective-permute-start(bf16[656,128]{1,0:T(8,128)(2,1)S(1)} %get-tuple-element.49), channel_id=1, source_target_pairs={{0,1},{1,0},{2,3},{3,2},{4,5},{5,4},{6,7},{7,6},{8,24},{9,25},{10,... | collective-permute-start | bytes 503816 | tf_op jit(solution)/shard_map/ppermute | solution.py:514
  92.4 2.0 %collective-permute-start.37 = (bf16[656,128]{1,0:T(8,128)(2,1)S(1)}, bf16[656,128]{1,0:T(8,128)(2,1)S(1)}, u32[]{:S(2)}, u32[]{:S(2)}) collective-permute-start(bf16[656,128]{1,0:T(8,128)(2,1)S(1)} %get-tuple-element.53), channel_id=1, source_target_pairs={{0,2},{1,3},{2,0},{3,1},{4,6},{5,7},{6,4},{7,5},{8,10},{9,11},{10,... | collective-permute-start | bytes 503816 | tf_op jit(solution)/shard_map/ppermute | solution.py:514
  96.3 1.7 %collective-permute-start.49 = (bf16[656,128]{1,0:T(8,128)(2,1)S(1)}, bf16[656,128]{1,0:T(8,128)(2,1)S(1)}, u32[]{:S(2)}, u32[]{:S(2)}) collective-permute-start(bf16[656,128]{1,0:T(8,128)(2,1)S(1)} %get-tuple-element.41), channel_id=1, source_target_pairs={{0,16},{1,17},{2,18},{3,19},{4,20},{5,21},{6,22},{7,23},{8,9},{9,8... | collective-permute-start | bytes 503816 | tf_op jit(solution)/shard_map/ppermute | solution.py:514
  98.0 3.8 %collective-permute-done.34 = bf16[656,128]{1,0:T(8,128)(2,1)S(1)} collective-permute-done((bf16[656,128]{1,0:T(8,128)(2,1)S(1)}, bf16[656,128]{1,0:T(8,128)(2,1)S(1)}, u32[]{:S(2)}, u32[]{:S(2)}) %collective-permute-start.34) | collective-permute-done | bytes 167968 | tf_op jit(solution)/shard_map/ppermute | solution.py:514
  101.8 1.7 %collective-permute-start.46 = (bf16[656,128]{1,0:T(8,128)(2,1)S(1)}, bf16[656,128]{1,0:T(8,128)(2,1)S(1)}, u32[]{:S(2)}, u32[]{:S(2)}) collective-permute-start(bf16[656,128]{1,0:T(8,128)(2,1)S(1)} %get-tuple-element.42), channel_id=1, source_target_pairs={{0,2},{1,3},{2,0},{3,1},{4,6},{5,7},{6,4},{7,5},{8,10},{9,11},{10,... | collective-permute-start | bytes 503816 | tf_op jit(solution)/shard_map/ppermute | solution.py:514
  104.5 2.7 %collective-permute-done.46.refs_2_ = bf16[656,128]{1,0:T(8,128)(2,1)S(1)} collective-permute-done((bf16[656,128]{1,0:T(8,128)(2,1)S(1)}, bf16[656,128]{1,0:T(8,128)(2,1)S(1)}, u32[]{:S(2)}, u32[]{:S(2)}) %collective-permute-start.46) | collective-permute-done | bytes 167968 | tf_op jit(solution)/shard_map/ppermute | solution.py:514
  107.2 4.7 %collective-permute-done.42.refs_1_ = bf16[656,128]{1,0:T(8,128)(2,1)S(1)} collective-permute-done((bf16[656,128]{1,0:T(8,128)(2,1)S(1)}, bf16[656,128]{1,0:T(8,128)(2,1)S(1)}, u32[]{:S(2)}, u32[]{:S(2)}) %collective-permute-start.42) | collective-permute-done | bytes 167968 | tf_op jit(solution)/shard_map/ppermute | solution.py:514
  114.3 1.6 %collective-permute-start.52 = (f32[8,128]{1,0:T(8,128)S(1)}, f32[8,128]{1,0:T(8,128)S(1)}, u32[]{:S(2)}, u32[]{:S(2)}) collective-permute-start(f32[8,128]{1,0:T(8,128)S(1)} %add.175), channel_id=1, source_target_pairs={{0,1},{1,0},{2,3},{3,2},{4,5},{5,4},{6,7},{7,6},{8,9},{9,8},{10,11... | collective-permute-start | bytes 12296 | tf_op jit(solution)/shard_map/ppermute | solution.py:580
  119.5 2.2 %collective-permute-start.56 = (f32[8,128]{1,0:T(8,128)S(1)}, f32[8,128]{1,0:T(8,128)S(1)}, u32[]{:S(2)}, u32[]{:S(2)}) collective-permute-start(f32[8,128]{1,0:T(8,128)S(1)} %add_add_fusion.1), channel_id=1, source_target_pairs={{0,6},{1,7},{2,4},{3,5},{4,2},{5,3},{6,0},{7,1},{8,14},{9,15},{10,... | collective-permute-start | bytes 12296 | tf_op jit(solution)/shard_map/ppermute | solution.py:580
  121.7 2.2 %collective-permute-start.54 = (f32[8,128]{1,0:T(8,128)S(1)}, f32[8,128]{1,0:T(8,128)S(1)}, u32[]{:S(2)}, u32[]{:S(2)}) collective-permute-start(f32[8,128]{1,0:T(8,128)S(1)} %add_add_fusion.1), channel_id=1, source_target_pairs={{0,2},{1,3},{2,0},{3,1},{4,6},{5,7},{6,4},{7,5},{8,10},{9,11},{10,... | collective-permute-start | bytes 12296 | tf_op jit(solution)/shard_map/ppermute | solution.py:580
  (114 shorter events, 35.6 us)
Async XLA Ops:
  2.4 8.2 %collective-permute-start.3 = (bf16[656,128]{1,0:T(8,128)(2,1)S(1)}, bf16[656,128]{1,0:T(8,128)(2,1)S(1)}, u32[]{:S(2)}, u32[]{:S(2)}) collective-permute-start(bf16[656,128]{1,0:T(8,128)(2,1)S(1)} %shift.1.rest_0_), channel_id=1, source_target_pairs={{0,16},{1,17},{2,18},{3,19},{4,20},{5,21},{6,22},{7,23},{8,9},{9,8... | collective-permute-start | bytes 503816 | tf_op jit(solution)/shard_map/ppermute | solution.py:514
  6.9 9.0 %collective-permute-start.1 = (bf16[656,128]{1,0:T(8,128)(2,1)S(1)}, bf16[656,128]{1,0:T(8,128)(2,1)S(1)}, u32[]{:S(2)}, u32[]{:S(2)}) collective-permute-start(bf16[656,128]{1,0:T(8,128)(2,1)S(1)} %shift.1.rest_0_), channel_id=1, source_target_pairs={{0,6},{1,7},{2,4},{3,5},{4,2},{5,3},{6,0},{7,1},{8,14},{9,15},{10,... | collective-permute-start | bytes 503816 | tf_op jit(solution)/shard_map/ppermute | solution.py:514
  10.5 9.3 %collective-permute-start = (bf16[656,128]{1,0:T(8,128)(2,1)S(1)}, bf16[656,128]{1,0:T(8,128)(2,1)S(1)}, u32[]{:S(2)}, u32[]{:S(2)}) collective-permute-start(bf16[656,128]{1,0:T(8,128)(2,1)S(1)} %shift.1.rest_0_), channel_id=1, source_target_pairs={{0,2},{1,3},{2,0},{3,1},{4,6},{5,7},{6,4},{7,5},{8,10},{9,11},{10,... | collective-permute-start | bytes 503816 | tf_op jit(solution)/shard_map/ppermute | solution.py:514
  10.5 9.3 %collective-permute-start.19 = (bf16[656,128]{1,0:T(8,128)(2,1)S(1)}, bf16[656,128]{1,0:T(8,128)(2,1)S(1)}, u32[]{:S(2)}, u32[]{:S(2)}) collective-permute-start(bf16[656,128]{1,0:T(8,128)(2,1)S(1)} %collective-permute-done.3.rest_4_), channel_id=1, source_target_pairs={{0,8},{1,9},{2,10},{3,11},{4,12},{5,13},{6,14},{7,15},{8,0},{9,1},... | collective-permute-start | bytes 503816 | tf_op jit(solution)/shard_map/ppermute | solution.py:514
  10.8 9.6 %collective-permute-start.18 = (bf16[656,128]{1,0:T(8,128)(2,1)S(1)}, bf16[656,128]{1,0:T(8,128)(2,1)S(1)}, u32[]{:S(2)}, u32[]{:S(2)}) collective-permute-start(bf16[656,128]{1,0:T(8,128)(2,1)S(1)} %collective-permute-done.2.rest_3_), channel_id=1, source_target_pairs={{0,8},{1,9},{2,10},{3,11},{4,12},{5,13},{6,14},{7,15},{8,0},{9,1},... | collective-permute-start | bytes 503816 | tf_op jit(solution)/shard_map/ppermute | solution.py:514
  11.1 10.3 %collective-permute-start.7 = (bf16[656,128]{1,0:T(8,128)(2,1)S(1)}, bf16[656,128]{1,0:T(8,128)(2,1)S(1)}, u32[]{:S(2)}, u32[]{:S(2)}) collective-permute-start(bf16[656,128]{1,0:T(8,128)(2,1)S(1)} %collective-permute-done.2.rest_3_), channel_id=1, source_target_pairs={{0,16},{1,17},{2,18},{3,19},{4,20},{5,21},{6,22},{7,23},{8,9},{9,8... | collective-permute-start | bytes 503816 | tf_op jit(solution)/shard_map/ppermute | solution.py:514
  15.9 11.7 %collective-permute-start.6 = (bf16[656,128]{1,0:T(8,128)(2,1)S(1)}, bf16[656,128]{1,0:T(8,128)(2,1)S(1)}, u32[]{:S(2)}, u32[]{:S(2)}) collective-permute-start(bf16[656,128]{1,0:T(8,128)(2,1)S(1)} %collective-permute-done.2.rest_3_), channel_id=1, source_target_pairs={{0,4},{1,5},{2,6},{3,7},{4,0},{5,1},{6,2},{7,3},{8,12},{9,13},{10,... | collective-permute-start | bytes 503816 | tf_op jit(solution)/shard_map/ppermute | solution.py:514
  19.8 7.8 %collective-permute-start.17 = (bf16[656,128]{1,0:T(8,128)(2,1)S(1)}, bf16[656,128]{1,0:T(8,128)(2,1)S(1)}, u32[]{:S(2)}, u32[]{:S(2)}) collective-permute-start(bf16[656,128]{1,0:T(8,128)(2,1)S(1)} %collective-permute-done.1.rest_2_), channel_id=1, source_target_pairs={{0,8},{1,9},{2,10},{3,11},{4,12},{5,13},{6,14},{7,15},{8,0},{9,1},... | collective-permute-start | bytes 503816 | tf_op jit(solution)/shard_map/ppermute | solution.py:514
  19.8 8.3 %collective-permute-start.11 = (bf16[656,128]{1,0:T(8,128)(2,1)S(1)}, bf16[656,128]{1,0:T(8,128)(2,1)S(1)}, u32[]{:S(2)}, u32[]{:S(2)}) collective-permute-start(bf16[656,128]{1,0:T(8,128)(2,1)S(1)} %collective-permute-done.1.rest_2_), channel_id=1, source_target_pairs={{0,1},{1,0},{2,3},{3,2},{4,5},{5,4},{6,7},{7,6},{8,24},{9,25},{10,... | collective-permute-start | bytes 503816 | tf_op jit(solution)/shard_map/ppermute | solution.py:514
  20.4 8.8 %collective-permute-start.9 = (bf16[656,128]{1,0:T(8,128)(2,1)S(1)}, bf16[656,128]{1,0:T(8,128)(2,1)S(1)}, u32[]{:S(2)}, u32[]{:S(2)}) collective-permute-start(bf16[656,128]{1,0:T(8,128)(2,1)S(1)} %collective-permute-done.1.rest_2_), channel_id=1, source_target_pairs={{0,2},{1,3},{2,0},{3,1},{4,6},{5,7},{6,4},{7,5},{8,10},{9,11},{10,... | collective-permute-start | bytes 503816 | tf_op jit(solution)/shard_map/ppermute | solution.py:514
  21.4 7.8 %collective-permute-start.8 = (bf16[656,128]{1,0:T(8,128)(2,1)S(1)}, bf16[656,128]{1,0:T(8,128)(2,1)S(1)}, u32[]{:S(2)}, u32[]{:S(2)}) collective-permute-start(bf16[656,128]{1,0:T(8,128)(2,1)S(1)} %collective-permute-done.1.rest_2_), channel_id=1, source_target_pairs={{0,16},{1,17},{2,18},{3,19},{4,20},{5,21},{6,22},{7,23},{8,9},{9,8... | collective-permute-start | bytes 503816 | tf_op jit(solution)/shard_map/ppermute | solution.py:514
  28.2 7.2 %collective-permute-start.4 = (bf16[656,128]{1,0:T(8,128)(2,1)S(1)}, bf16[656,128]{1,0:T(8,128)(2,1)S(1)}, u32[]{:S(2)}, u32[]{:S(2)}) collective-permute-start(bf16[656,128]{1,0:T(8,128)(2,1)S(1)} %collective-permute-done.rest_1_), channel_id=1, source_target_pairs={{0,1},{1,0},{2,3},{3,2},{4,5},{5,4},{6,7},{7,6},{8,24},{9,25},{10,... | collective-permute-start | bytes 503816 | tf_op jit(solution)/shard_map/ppermute | solution.py:514
  73.1 17.2 %collective-permute-start.31 = (bf16[4,656,128]{2,1,0:T(8,128)(2,1)S(1)}, bf16[4,656,128]{2,1,0:T(8,128)(2,1)S(1)}, u32[]{:S(2)}, u32[]{:S(2)}) collective-permute-start(bf16[4,656,128]{2,1,0:T(8,128)(2,1)S(1)} %get-tuple-element.28), channel_id=1, source_target_pairs={{0,8},{1,9},{2,10},{3,11},{4,12},{5,13},{6,14},{7,15},{8,0},{9,1},... | collective-permute-start | bytes 2015240 | tf_op jit(solution)/shard_map/ppermute | solution.py:514
  73.3 11.0 %collective-permute-start.32 = (bf16[4,656,128]{2,1,0:T(8,128)(2,1)S(1)}, bf16[4,656,128]{2,1,0:T(8,128)(2,1)S(1)}, u32[]{:S(2)}, u32[]{:S(2)}) collective-permute-start(bf16[4,656,128]{2,1,0:T(8,128)(2,1)S(1)} %get-tuple-element.30), channel_id=1, source_target_pairs={{0,8},{1,9},{2,10},{3,11},{4,12},{5,13},{6,14},{7,15},{8,0},{9,1},... | collective-permute-start | bytes 2015240 | tf_op jit(solution)/shard_map/ppermute | solution.py:514
  74.8 7.2 %collective-permute-start.39 = (bf16[656,128]{1,0:T(8,128)(2,1)S(1)}, bf16[656,128]{1,0:T(8,128)(2,1)S(1)}, u32[]{:S(2)}, u32[]{:S(2)}) collective-permute-start(bf16[656,128]{1,0:T(8,128)(2,1)S(1)} %get-tuple-element.50), channel_id=1, source_target_pairs={{0,2},{1,3},{2,0},{3,1},{4,6},{5,7},{6,4},{7,5},{8,10},{9,11},{10,... | collective-permute-start | bytes 503816 | tf_op jit(solution)/shard_map/ppermute | solution.py:514
  76.7 8.3 %collective-permute-start.38 = (bf16[656,128]{1,0:T(8,128)(2,1)S(1)}, bf16[656,128]{1,0:T(8,128)(2,1)S(1)}, u32[]{:S(2)}, u32[]{:S(2)}) collective-permute-start(bf16[656,128]{1,0:T(8,128)(2,1)S(1)} %get-tuple-element.51), channel_id=1, source_target_pairs={{0,2},{1,3},{2,0},{3,1},{4,6},{5,7},{6,4},{7,5},{8,10},{9,11},{10,... | collective-permute-start | bytes 503816 | tf_op jit(solution)/shard_map/ppermute | solution.py:514
  84.4 8.0 %collective-permute-start.48 = (bf16[656,128]{1,0:T(8,128)(2,1)S(1)}, bf16[656,128]{1,0:T(8,128)(2,1)S(1)}, u32[]{:S(2)}, u32[]{:S(2)}) collective-permute-start(bf16[656,128]{1,0:T(8,128)(2,1)S(1)} %fusion.27), channel_id=1, source_target_pairs={{0,1},{1,0},{2,3},{3,2},{4,5},{5,4},{6,7},{7,6},{8,24},{9,25},{10,... | collective-permute-start | bytes 503816 | tf_op jit(solution)/shard_map/ppermute | solution.py:514
  85.0 10.8 %collective-permute-start.43 = (bf16[656,128]{1,0:T(8,128)(2,1)S(1)}, bf16[656,128]{1,0:T(8,128)(2,1)S(1)}, u32[]{:S(2)}, u32[]{:S(2)}) collective-permute-start(bf16[656,128]{1,0:T(8,128)(2,1)S(1)} %get-tuple-element.45), channel_id=1, source_target_pairs={{0,1},{1,0},{2,3},{3,2},{4,5},{5,4},{6,7},{7,6},{8,24},{9,25},{10,... | collective-permute-start | bytes 503816 | tf_op jit(solution)/shard_map/ppermute | solution.py:514
  90.3 14.2 %collective-permute-start.47 = (bf16[656,128]{1,0:T(8,128)(2,1)S(1)}, bf16[656,128]{1,0:T(8,128)(2,1)S(1)}, u32[]{:S(2)}, u32[]{:S(2)}) collective-permute-start(bf16[656,128]{1,0:T(8,128)(2,1)S(1)} %get-tuple-element.43), channel_id=1, source_target_pairs={{0,1},{1,0},{2,3},{3,2},{4,5},{5,4},{6,7},{7,6},{8,24},{9,25},{10,... | collective-permute-start | bytes 503816 | tf_op jit(solution)/shard_map/ppermute | solution.py:514
  90.8 11.0 %collective-permute-start.34 = (bf16[656,128]{1,0:T(8,128)(2,1)S(1)}, bf16[656,128]{1,0:T(8,128)(2,1)S(1)}, u32[]{:S(2)}, u32[]{:S(2)}) collective-permute-start(bf16[656,128]{1,0:T(8,128)(2,1)S(1)} %get-tuple-element.49), channel_id=1, source_target_pairs={{0,1},{1,0},{2,3},{3,2},{4,5},{5,4},{6,7},{7,6},{8,24},{9,25},{10,... | collective-permute-start | bytes 503816 | tf_op jit(solution)/shard_map/ppermute | solution.py:514
  92.4 11.2 %collective-permute-start.37 = (bf16[656,128]{1,0:T(8,128)(2,1)S(1)}, bf16[656,128]{1,0:T(8,128)(2,1)S(1)}, u32[]{:S(2)}, u32[]{:S(2)}) collective-permute-start(bf16[656,128]{1,0:T(8,128)(2,1)S(1)} %get-tuple-element.53), channel_id=1, source_target_pairs={{0,2},{1,3},{2,0},{3,1},{4,6},{5,7},{6,4},{7,5},{8,10},{9,11},{10,... | collective-permute-start | bytes 503816 | tf_op jit(solution)/shard_map/ppermute | solution.py:514
  95.8 7.8 %collective-permute-start.41 = (bf16[656,128]{1,0:T(8,128)(2,1)S(1)}, bf16[656,128]{1,0:T(8,128)(2,1)S(1)}, u32[]{:S(2)}, u32[]{:S(2)}) collective-permute-start(bf16[656,128]{1,0:T(8,128)(2,1)S(1)} %get-tuple-element.48), channel_id=1, source_target_pairs={{0,16},{1,17},{2,18},{3,19},{4,20},{5,21},{6,22},{7,23},{8,9},{9,8... | collective-permute-start | bytes 503816 | tf_op jit(solution)/shard_map/ppermute | solution.py:514
  96.3 8.2 %collective-permute-start.49 = (bf16[656,128]{1,0:T(8,128)(2,1)S(1)}, bf16[656,128]{1,0:T(8,128)(2,1)S(1)}, u32[]{:S(2)}, u32[]{:S(2)}) collective-permute-start(bf16[656,128]{1,0:T(8,128)(2,1)S(1)} %get-tuple-element.41), channel_id=1, source_target_pairs={{0,16},{1,17},{2,18},{3,19},{4,20},{5,21},{6,22},{7,23},{8,9},{9,8... | collective-permute-start | bytes 503816 | tf_op jit(solution)/shard_map/ppermute | solution.py:514
  103.7 8.1 %collective-permute-start.42 = (bf16[656,128]{1,0:T(8,128)(2,1)S(1)}, bf16[656,128]{1,0:T(8,128)(2,1)S(1)}, u32[]{:S(2)}, u32[]{:S(2)}) collective-permute-start(bf16[656,128]{1,0:T(8,128)(2,1)S(1)} %fusion.11), channel_id=1, source_target_pairs={{0,4},{1,5},{2,6},{3,7},{4,0},{5,1},{6,2},{7,3},{8,12},{9,13},{10,... | collective-permute-start | bytes 503816 | tf_op jit(solution)/shard_map/ppermute | solution.py:514
  (36 other events, 201.2 us)
